TPU v7x, 512 devices: a whole 4x4x16 slice. The times are simulated.
512 devices in a mesh: blk: 64 (over y, z_lo, core), lay: 8 (over z_hi, x).
Axes of the slice: x: 4, y: 4, z: 16 (z_hi: 2, z_lo: 8; z = z_hi * 8 + z_lo), core: 2. Of those that a mesh axis runs over, the one named last changes fastest.
Arguments:
- spectra: bfloat16 [2, 256, 4, 1024], P(None, 'blk'), may hold values from -6 to 6
- model_corr: bfloat16 [64, 32, 4, 4, 1024], P('blk', 'lay'), may hold values from -6 to 6
- window_start: int32 [64, 32], P('blk', 'lay'), may hold values from 0 to 511
- window_end: int32 [64, 32], P('blk', 'lay'), may hold values from 513 to 1024
- station_slot: int32 [64, 4], P('blk'), may hold values from 0 to 3, each once within a row
Outputs:
- adjoint: float32 [2, 256, 4, 1024], P(None, 'blk', None, 'lay')
Inputs may be any that keep to these rules, and one draw needn't show every extreme that they name: `station_slot`: each row lists every number from 0 to 3 once. `window_start`: every taper starts before the middle lag sample. `window_end`: every taper ends after the middle lag sample.
All inputs are finite; a program needn't handle non-finite values.
Results may differ from a plain program's by a relative error of at most 0.0022.
Values may be sent and summed in bfloat16 or wider, within the bound.
A program may use at most 64 MiB of HBM per device.

v0:
```python
import math

import jax
import jax.numpy as jnp
from jax import lax
from jax.sharding import PartitionSpec as P


def from_behind(value, axis, steps):
    count = lax.axis_size(axis)
    pairs = [(source, (source + steps) % count) for source in range(count)]
    return lax.ppermute(value, axis, pairs)


def lag_table(freq_count, lag_count, window_count):
    freq_index = jnp.arange(freq_count, dtype=jnp.int32)
    lag_index = jnp.arange(lag_count, dtype=jnp.int32) - lag_count // 2
    phase_index = freq_index[:, None] * lag_index[None, :] % (2 * freq_count)
    angle = phase_index.astype(jnp.float32) * (math.pi / freq_count)
    factor = 1.0 / math.sqrt(2.0 * freq_count * window_count)
    cosine = (jnp.cos(angle) * factor).astype(jnp.bfloat16)
    sine = (-jnp.sin(angle) * factor).astype(jnp.bfloat16)
    return jnp.concatenate([cosine, sine], axis=0)


def cross_of(ordered, partner):
    first = ordered.astype(jnp.float32)
    second = partner.astype(jnp.float32)
    cross_re = jnp.sum(
        first[0][:, None] * second[0][None] + first[1][:, None] * second[1][None], axis=2
    )
    cross_im = jnp.sum(
        first[1][:, None] * second[0][None] - first[0][:, None] * second[1][None], axis=2
    )
    return jnp.concatenate([cross_re.astype(jnp.bfloat16), cross_im.astype(jnp.bfloat16)], axis=2)


def terms_of(response, ordered, partner):
    freq_count = ordered.shape[3]
    first = ordered.astype(jnp.float32)
    second = partner.astype(jnp.float32)
    resp = response.astype(jnp.float32)
    resp_re = resp[:, :, None, :freq_count]
    resp_im = resp[:, :, None, freq_count:]
    own_re = jnp.sum(resp_re * second[0][None] - resp_im * second[1][None], axis=1)
    own_im = jnp.sum(resp_re * second[1][None] + resp_im * second[0][None], axis=1)
    part_re = jnp.sum(resp_re * first[0][:, None] + resp_im * first[1][:, None], axis=0)
    part_im = jnp.sum(resp_re * first[1][:, None] - resp_im * first[0][:, None], axis=0)
    return (jnp.stack([own_re, own_im]), jnp.stack([part_re, part_im]))


def local(spectra, model_corr, window_start, window_end, station_slot):
    station_count = spectra.shape[1]
    window_count = spectra.shape[2]
    freq_count = spectra.shape[3]
    offset_count = model_corr.shape[1]
    lag_count = model_corr.shape[4]
    layer_count = lax.axis_size("lay")
    block_count = lax.axis_size("blk")
    layer_index = lax.axis_index("lay")
    base_offset = layer_index * offset_count
    placing = (
        station_slot[0][:, None] == jnp.arange(station_count, dtype=jnp.int32)[None, :]
    ).astype(jnp.float32)
    ordered = jnp.sum(
        placing[None, :, :, None, None] * spectra.astype(jnp.float32)[:, None], axis=2
    ).astype(jnp.bfloat16)
    table = lag_table(freq_count, lag_count, window_count)
    bit_total = (layer_count - 1).bit_length()
    partner = ordered
    for bit_place in range(bit_total):
        shifted = from_behind(partner, "blk", -(offset_count << bit_place))
        partner = jnp.where((layer_index >> bit_place) % 2 == 1, shifted, partner)
    partners = []
    crosses = []
    for step_index in range(offset_count):
        partners.append(partner)
        crosses.append(cross_of(ordered, partner))
        if step_index + 1 < offset_count:
            partner = from_behind(partner, "blk", -1)
    pair_rows = station_count * station_count
    cross_all = jnp.stack(crosses).reshape(-1, 2 * freq_count)
    lagged = jnp.dot(cross_all, table, preferred_element_type=jnp.float32).reshape(
        offset_count, pair_rows, lag_count
    )
    lag_pos = jnp.arange(lag_count, dtype=jnp.int32)
    inside = (lag_pos[None, :] >= window_start[0][:, None]) & (
        lag_pos[None, :] < window_end[0][:, None]
    )
    station_pos = jnp.arange(station_count, dtype=jnp.int32)
    diagonal = (station_pos[:, None] == station_pos[None, :]).reshape(-1)
    offsets = base_offset + jnp.arange(offset_count, dtype=jnp.int32)
    paired = jnp.logical_not((offsets[:, None] == 0) & diagonal[None, :])
    keep = paired[:, :, None] & inside[:, None, :]
    model_rows = model_corr[0].reshape(offset_count, pair_rows, lag_count).astype(jnp.float32)
    misfit = jnp.where(keep, lagged - model_rows, 0.0).astype(jnp.bfloat16).reshape(-1, lag_count)
    response = lax.dot_general(
        misfit, table, (((1,), (1,)), ((), ())), preferred_element_type=jnp.float32
    )
    response = response.astype(jnp.bfloat16).reshape(
        offset_count, station_count, station_count, 2 * freq_count
    )
    own_sum = jnp.zeros((2, station_count, window_count, freq_count), jnp.float32)
    carried = jnp.zeros((2, station_count, window_count, freq_count), jnp.float32)
    for step_index in range(offset_count):
        own_side, partner_side = terms_of(response[step_index], ordered, partners[step_index])
        own_sum = own_sum + own_side
        carried = carried + partner_side
        if step_index + 1 < offset_count:
            carried = from_behind(carried, "blk", -1)
    home_sum = from_behind(carried, "blk", offset_count - 1)
    for bit_place in range(bit_total):
        shifted = from_behind(home_sum, "blk", offset_count << bit_place)
        home_sum = jnp.where((layer_index >> bit_place) % 2 == 1, shifted, home_sum)
    combined = own_sum + home_sum
    reduced = lax.psum_scatter(combined, "lay", scatter_dimension=3, tiled=True)
    scaled = reduced * (1.0 / math.sqrt(block_count * station_count))
    return jnp.sum(placing[None, :, :, None, None] * scaled[:, :, None], axis=1)


def solution(mesh):
    in_specs = (
        P(None, "blk", None, None),
        P("blk", "lay", None, None, None),
        P("blk", "lay"),
        P("blk", "lay"),
        P("blk", None),
    )
    out_specs = P(None, "blk", None, "lay")
    return jax.shard_map(local, mesh=mesh, in_specs=in_specs, out_specs=out_specs, check_vma=False)
```

profile of v0, /device:TPU:1, one launch (start us, length us, event | category | flops | bytes accessed | tf_op | source)
XLA Modules:
  0.0 323.8 jit_solution(17768336663802541463)
XLA Ops:
  8.4 14.8 %collective-permute-start = (bf16[2,4,4,1024]{3,2,1,0:T(4,128)(2,1)S(1)}, bf16[2,4,4,1024]{3,2,1,0:T(4,128)(2,1)S(1)}, u32[]{:S(2)}, u32[]{:S(2)}) collective-permute-start(bf16[2,4,4,1024]{3,2,1,0:T(4,128)(2,1)S(1)} %multiply_reduce_fusion), channel_id=1, source_target_pairs={{0,480},{8,488},{16,496},{24,504},{32,0},{40,8},{48,16},{56,24},{6... | collective-permute-start | bytes 196616 | tf_op jit(solution)/shard_map/ppermute | solution.py:12
  23.3 18.2 %multiply_convert_fusion.1 = (bf16[1024,1024]{1,0:T(8,128)(2,1)S(1)}, bf16[1024,1024]{1,0:T(8,128)(2,1)}) fusion(s32[1024]{0:T(1024)S(1)} %iota_add_fusion), kind=kLoop, calls=%fused_computation.10 | loop fusion | flops 19922944 | bytes 4198400 | tf_op jit(solution)/shard_map/convert_element_type | solution.py:21
  41.6 1.9 collective-permute-start.1
  43.7 6.9 %collective-permute-done.1 = bf16[2,4,4,1024]{3,2,1,0:T(4,128)(2,1)S(1)} collective-permute-done((bf16[2,4,4,1024]{3,2,1,0:T(4,128)(2,1)S(1)}, bf16[2,4,4,1024]{3,2,1,0:T(4,128)(2,1)S(1)}, u32[]{:S(2)}, u32[]{:S(2)}) %collective-permute-start.1) | collective-permute-done | bytes 65568 | tf_op jit(solution)/shard_map/ppermute | solution.py:12
  50.6 2.4 collective-permute-start.2
  53.0 2.6 collective-permute-done.2
  55.6 5.8 %collective-permute-start.3 = (bf16[2,4,4,1024]{3,2,1,0:T(4,128)(2,1)S(1)}, bf16[2,4,4,1024]{3,2,1,0:T(4,128)(2,1)S(1)}, u32[]{:S(2)}, u32[]{:S(2)}) collective-permute-start(bf16[2,4,4,1024]{3,2,1,0:T(4,128)(2,1)S(1)} %get-tuple-element.50), channel_id=1, source_target_pairs={{0,504},{8,0},{16,8},{24,16},{32,24},{40,32},{48,40},{56,48},{64,5... | collective-permute-start | bytes 196616 | tf_op jit(solution)/shard_map/ppermute | solution.py:12
  61.5 2.8 collective-permute-done.3
  64.3 6.5 %collective-permute-start.4 = (bf16[2,4,4,1024]{3,2,1,0:T(4,128)(2,1)S(1)}, bf16[2,4,4,1024]{3,2,1,0:T(4,128)(2,1)S(1)}, u32[]{:S(2)}, u32[]{:S(2)}) collective-permute-start(bf16[2,4,4,1024]{3,2,1,0:T(4,128)(2,1)S(1)} %collective-permute-done.3), channel_id=1, source_target_pairs={{0,504},{8,0},{16,8},{24,16},{32,24},{40,32},{48,40},{56,48},{64,5... | collective-permute-start | bytes 196616 | tf_op jit(solution)/shard_map/ppermute | solution.py:12
  71.6 13.4 %collective-permute-start.5 = (bf16[2,4,4,1024]{3,2,1,0:T(4,128)(2,1)S(1)}, bf16[2,4,4,1024]{3,2,1,0:T(4,128)(2,1)S(1)}, u32[]{:S(2)}, u32[]{:S(2)}) collective-permute-start(bf16[2,4,4,1024]{3,2,1,0:T(4,128)(2,1)S(1)} %collective-permute-done.4), channel_id=1, source_target_pairs={{0,504},{8,0},{16,8},{24,16},{32,24},{40,32},{48,40},{56,48},{64,5... | collective-permute-start | bytes 196616 | tf_op jit(solution)/shard_map/ppermute | solution.py:12
  85.9 1.7 add_reduce_fusion.11
  87.8 2.6 fusion.16
  90.4 1.4 fusion.9
  92.1 1.6 add_reduce_fusion
  93.8 13.4 %collective-permute-start.6 = (f32[2,4,4,1024]{3,2,1,0:T(4,128)S(1)}, f32[2,4,4,1024]{3,2,1,0:T(4,128)S(1)}, u32[]{:S(2)}, u32[]{:S(2)}) collective-permute-start(f32[2,4,4,1024]{3,2,1,0:T(4,128)S(1)} %pad_maximum_fusion.5), channel_id=1, source_target_pairs={{0,504},{8,0},{16,8},{24,16},{32,24},{40,32},{48,40},{56,48},{64,5... | collective-permute-start | bytes 393224 | tf_op jit(solution)/shard_map/ppermute | solution.py:12
  107.2 1.0 collective-permute-done.6
  108.2 13.9 %collective-permute-start.7 = (f32[2,4,4,1024]{3,2,1,0:T(4,128)S(1)}, f32[2,4,4,1024]{3,2,1,0:T(4,128)S(1)}, u32[]{:S(2)}, u32[]{:S(2)}) collective-permute-start(f32[2,4,4,1024]{3,2,1,0:T(4,128)S(1)} %maximum_add_fusion.1), channel_id=1, source_target_pairs={{0,504},{8,0},{16,8},{24,16},{32,24},{40,32},{48,40},{56,48},{64,5... | collective-permute-start | bytes 393224 | tf_op jit(solution)/shard_map/ppermute | solution.py:12
  122.1 1.0 collective-permute-done.7
  123.2 14.1 %collective-permute-start.8 = (f32[2,4,4,1024]{3,2,1,0:T(4,128)S(1)}, f32[2,4,4,1024]{3,2,1,0:T(4,128)S(1)}, u32[]{:S(2)}, u32[]{:S(2)}) collective-permute-start(f32[2,4,4,1024]{3,2,1,0:T(4,128)S(1)} %maximum_add_fusion.2), channel_id=1, source_target_pairs={{0,504},{8,0},{16,8},{24,16},{32,24},{40,32},{48,40},{56,48},{64,5... | collective-permute-start | bytes 393224 | tf_op jit(solution)/shard_map/ppermute | solution.py:12
  137.3 1.0 collective-permute-done.8
  138.3 1.9 collective-permute-start.9
  140.2 13.1 %collective-permute-done.9 = f32[2,4,4,1024]{3,2,1,0:T(4,128)S(1)} collective-permute-done((f32[2,4,4,1024]{3,2,1,0:T(4,128)S(1)}, f32[2,4,4,1024]{3,2,1,0:T(4,128)S(1)}, u32[]{:S(2)}, u32[]{:S(2)}) %collective-permute-start.9) | collective-permute-done | bytes 131104 | tf_op jit(solution)/shard_map/ppermute | solution.py:12
  153.3 1.9 collective-permute-start.10
  155.2 13.8 %collective-permute-done.10 = f32[2,4,4,1024]{3,2,1,0:T(4,128)S(1)} collective-permute-done((f32[2,4,4,1024]{3,2,1,0:T(4,128)S(1)}, f32[2,4,4,1024]{3,2,1,0:T(4,128)S(1)}, u32[]{:S(2)}, u32[]{:S(2)}) %collective-permute-start.10) | collective-permute-done | bytes 131104 | tf_op jit(solution)/shard_map/ppermute | solution.py:12
  169.1 1.9 collective-permute-start.11
  171.0 14.0 %collective-permute-done.11 = f32[2,4,4,1024]{3,2,1,0:T(4,128)S(1)} collective-permute-done((f32[2,4,4,1024]{3,2,1,0:T(4,128)S(1)}, f32[2,4,4,1024]{3,2,1,0:T(4,128)S(1)}, u32[]{:S(2)}, u32[]{:S(2)}) %collective-permute-start.11) | collective-permute-done | bytes 131104 | tf_op jit(solution)/shard_map/ppermute | solution.py:12
  185.0 1.9 collective-permute-start.12
  187.0 5.0 %collective-permute-done.12 = f32[2,4,4,1024]{3,2,1,0:T(4,128)S(1)} collective-permute-done((f32[2,4,4,1024]{3,2,1,0:T(4,128)S(1)}, f32[2,4,4,1024]{3,2,1,0:T(4,128)S(1)}, u32[]{:S(2)}, u32[]{:S(2)}) %collective-permute-start.12) | collective-permute-done | bytes 131104 | tf_op jit(solution)/shard_map/ppermute | solution.py:12
  192.1 3.2 copy.6
  195.3 4.9 %reshape.218 = f32[1024,32]{1,0:T(8,128)} reshape(f32[1024,2,4,4]{3,2,1,0:T(4,128)} %bitcast.61) | data formatting | bytes 262144
  200.2 114.6 %reduce-scatter.4.cloned.1.call-done = f32[128,32]{1,0:T(8,128)} async-done(((f32[1024,32]{1,0:T(8,128)}), f32[128,32]{1,0:T(8,128)}) %reduce-scatter.4.cloned.1.call-update) | async-done | bytes 16400
  314.7 1.2 reshape.219
  (59 shorter events, 5.6 us)
Async XLA Ops:
  6.5 35.0 %copy-start.2 = (s32[1,4]{1,0:T(1,128)S(1)}, s32[1,4]{1,0:T(1,128)}, u32[]{:S(2)}) copy-start(s32[1,4]{1,0:T(1,128)} %param.8) | copy-start | bytes 52
  6.5 35.0 %copy-start.3 = (s32[1,4]{1,0:T(1,128)S(1)}, s32[1,4]{1,0:T(1,128)}, u32[]{:S(2)}) copy-start(s32[1,4]{1,0:T(1,128)} %param.7) | copy-start | bytes 52
  6.5 37.1 %copy-start.1 = (bf16[1,4,4,4,1024]{4,3,2,1,0:T(4,128)(2,1)S(1)}, bf16[1,4,4,4,1024]{4,3,2,1,0:T(4,128)(2,1)}, u32[]{:S(2)}) copy-start(bf16[1,4,4,4,1024]{4,3,2,1,0:T(4,128)(2,1)} %param.6) | copy-start | bytes 393220
  6.5 308.2 %reduce-scatter.4.cloned.1.call-start = ((), (), s32[]{:S(2)}) async-start(), calls=%async_computation.1 | async-start | bytes 589824
  8.4 33.2 %collective-permute-start = (bf16[2,4,4,1024]{3,2,1,0:T(4,128)(2,1)S(1)}, bf16[2,4,4,1024]{3,2,1,0:T(4,128)(2,1)S(1)}, u32[]{:S(2)}, u32[]{:S(2)}) collective-permute-start(bf16[2,4,4,1024]{3,2,1,0:T(4,128)(2,1)S(1)} %multiply_reduce_fusion), channel_id=1, source_target_pairs={{0,480},{8,488},{16,496},{24,504},{32,0},{40,8},{48,16},{56,24},{6... | collective-permute-start | bytes 196616 | tf_op jit(solution)/shard_map/ppermute | solution.py:12
  41.6 8.9 %collective-permute-start.1 = (bf16[2,4,4,1024]{3,2,1,0:T(4,128)(2,1)S(1)}, bf16[2,4,4,1024]{3,2,1,0:T(4,128)(2,1)S(1)}, u32[]{:S(2)}, u32[]{:S(2)}) collective-permute-start(bf16[2,4,4,1024]{3,2,1,0:T(4,128)(2,1)S(1)} %get-tuple-element.74), channel_id=1, source_target_pairs={{0,448},{8,456},{16,464},{24,472},{32,480},{40,488},{48,496},{56,5... | collective-permute-start | bytes 196616 | tf_op jit(solution)/shard_map/ppermute | solution.py:12
  50.6 5.0 %collective-permute-start.2 = (bf16[2,4,4,1024]{3,2,1,0:T(4,128)(2,1)S(1)}, bf16[2,4,4,1024]{3,2,1,0:T(4,128)(2,1)S(1)}, u32[]{:S(2)}, u32[]{:S(2)}) collective-permute-start(bf16[2,4,4,1024]{3,2,1,0:T(4,128)(2,1)S(1)} %bitcast.75), channel_id=1, source_target_pairs={{0,384},{8,392},{16,400},{24,408},{32,416},{40,424},{48,432},{56,4... | collective-permute-start | bytes 196616 | tf_op jit(solution)/shard_map/ppermute | solution.py:12
  55.6 8.6 %collective-permute-start.3 = (bf16[2,4,4,1024]{3,2,1,0:T(4,128)(2,1)S(1)}, bf16[2,4,4,1024]{3,2,1,0:T(4,128)(2,1)S(1)}, u32[]{:S(2)}, u32[]{:S(2)}) collective-permute-start(bf16[2,4,4,1024]{3,2,1,0:T(4,128)(2,1)S(1)} %get-tuple-element.50), channel_id=1, source_target_pairs={{0,504},{8,0},{16,8},{24,16},{32,24},{40,32},{48,40},{56,48},{64,5... | collective-permute-start | bytes 196616 | tf_op jit(solution)/shard_map/ppermute | solution.py:12
  64.3 7.4 %collective-permute-start.4 = (bf16[2,4,4,1024]{3,2,1,0:T(4,128)(2,1)S(1)}, bf16[2,4,4,1024]{3,2,1,0:T(4,128)(2,1)S(1)}, u32[]{:S(2)}, u32[]{:S(2)}) collective-permute-start(bf16[2,4,4,1024]{3,2,1,0:T(4,128)(2,1)S(1)} %collective-permute-done.3), channel_id=1, source_target_pairs={{0,504},{8,0},{16,8},{24,16},{32,24},{40,32},{48,40},{56,48},{64,5... | collective-permute-start | bytes 196616 | tf_op jit(solution)/shard_map/ppermute | solution.py:12
  71.6 14.3 %collective-permute-start.5 = (bf16[2,4,4,1024]{3,2,1,0:T(4,128)(2,1)S(1)}, bf16[2,4,4,1024]{3,2,1,0:T(4,128)(2,1)S(1)}, u32[]{:S(2)}, u32[]{:S(2)}) collective-permute-start(bf16[2,4,4,1024]{3,2,1,0:T(4,128)(2,1)S(1)} %collective-permute-done.4), channel_id=1, source_target_pairs={{0,504},{8,0},{16,8},{24,16},{32,24},{40,32},{48,40},{56,48},{64,5... | collective-permute-start | bytes 196616 | tf_op jit(solution)/shard_map/ppermute | solution.py:12
  87.8 2.6 copy-start
  93.8 14.4 %collective-permute-start.6 = (f32[2,4,4,1024]{3,2,1,0:T(4,128)S(1)}, f32[2,4,4,1024]{3,2,1,0:T(4,128)S(1)}, u32[]{:S(2)}, u32[]{:S(2)}) collective-permute-start(f32[2,4,4,1024]{3,2,1,0:T(4,128)S(1)} %pad_maximum_fusion.5), channel_id=1, source_target_pairs={{0,504},{8,0},{16,8},{24,16},{32,24},{40,32},{48,40},{56,48},{64,5... | collective-permute-start | bytes 393224 | tf_op jit(solution)/shard_map/ppermute | solution.py:12
  108.2 14.9 %collective-permute-start.7 = (f32[2,4,4,1024]{3,2,1,0:T(4,128)S(1)}, f32[2,4,4,1024]{3,2,1,0:T(4,128)S(1)}, u32[]{:S(2)}, u32[]{:S(2)}) collective-permute-start(f32[2,4,4,1024]{3,2,1,0:T(4,128)S(1)} %maximum_add_fusion.1), channel_id=1, source_target_pairs={{0,504},{8,0},{16,8},{24,16},{32,24},{40,32},{48,40},{56,48},{64,5... | collective-permute-start | bytes 393224 | tf_op jit(solution)/shard_map/ppermute | solution.py:12
  123.2 15.1 %collective-permute-start.8 = (f32[2,4,4,1024]{3,2,1,0:T(4,128)S(1)}, f32[2,4,4,1024]{3,2,1,0:T(4,128)S(1)}, u32[]{:S(2)}, u32[]{:S(2)}) collective-permute-start(f32[2,4,4,1024]{3,2,1,0:T(4,128)S(1)} %maximum_add_fusion.2), channel_id=1, source_target_pairs={{0,504},{8,0},{16,8},{24,16},{32,24},{40,32},{48,40},{56,48},{64,5... | collective-permute-start | bytes 393224 | tf_op jit(solution)/shard_map/ppermute | solution.py:12
  138.3 15.0 %collective-permute-start.9 = (f32[2,4,4,1024]{3,2,1,0:T(4,128)S(1)}, f32[2,4,4,1024]{3,2,1,0:T(4,128)S(1)}, u32[]{:S(2)}, u32[]{:S(2)}) collective-permute-start(f32[2,4,4,1024]{3,2,1,0:T(4,128)S(1)} %maximum_add_fusion.3), channel_id=1, source_target_pairs={{0,24},{8,32},{16,40},{24,48},{32,56},{40,64},{48,72},{56,80},{64,... | collective-permute-start | bytes 393224 | tf_op jit(solution)/shard_map/ppermute | solution.py:12
  153.3 15.7 %collective-permute-start.10 = (f32[2,4,4,1024]{3,2,1,0:T(4,128)S(1)}, f32[2,4,4,1024]{3,2,1,0:T(4,128)S(1)}, u32[]{:S(2)}, u32[]{:S(2)}) collective-permute-start(f32[2,4,4,1024]{3,2,1,0:T(4,128)S(1)} %collective-permute-done.9), channel_id=1, source_target_pairs={{0,32},{8,40},{16,48},{24,56},{32,64},{40,72},{48,80},{56,88},{64,... | collective-permute-start | bytes 393224 | tf_op jit(solution)/shard_map/ppermute | solution.py:12
  169.1 15.9 %collective-permute-start.11 = (f32[2,4,4,1024]{3,2,1,0:T(4,128)S(1)}, f32[2,4,4,1024]{3,2,1,0:T(4,128)S(1)}, u32[]{:S(2)}, u32[]{:S(2)}) collective-permute-start(f32[2,4,4,1024]{3,2,1,0:T(4,128)S(1)} %bitcast.65), channel_id=1, source_target_pairs={{0,64},{8,72},{16,80},{24,88},{32,96},{40,104},{48,112},{56,120},{... | collective-permute-start | bytes 393224 | tf_op jit(solution)/shard_map/ppermute | solution.py:12
  185.0 6.9 %collective-permute-start.12 = (f32[2,4,4,1024]{3,2,1,0:T(4,128)S(1)}, f32[2,4,4,1024]{3,2,1,0:T(4,128)S(1)}, u32[]{:S(2)}, u32[]{:S(2)}) collective-permute-start(f32[2,4,4,1024]{3,2,1,0:T(4,128)S(1)} %bitcast.63), channel_id=1, source_target_pairs={{0,128},{8,136},{16,144},{24,152},{32,160},{40,168},{48,176},{56,1... | collective-permute-start | bytes 393224 | tf_op jit(solution)/shard_map/ppermute | solution.py:12
Sparse Core Ops, SparseCore 0:
  200.3 114.3 reduce-scatter.3
where the time goes:
time: 325 us; the launch traced here: 324 us
  waiting for transfers between devices  177 us (54%)
  starting transfers between devices  93.9 us (29%)
  other arithmetic  24.7 us (8%)
  between operations  13.8 us (4%)
  local copies, waits for them, and re-layouts  10 us (3%)
  matrix products  3.99 us (1%)
    unnamed x2, waiting for transfers between devices  115 us
    ppermute x13, starting transfers between devices, from_behind(): return lax.ppermute(value, axis, pairs)  93.9 us
    ppermute x13, waiting for transfers between devices, from_behind(): return lax.ppermute(value, axis, pairs)  62.8 us
    convert_element_type x1, other arithmetic, lag_table(): cosine = (jnp.cos(angle) * factor).astype(jnp.bfloat16)  18.2 us
    unnamed x12, local copies, waits for them, and re-layouts  9.52 us
  transfers between devices with their start and end apart: 14, of which 13 were waited for; matrix products, arithmetic and copies ran while one was open for 6% of the time, Pallas kernels for 0%

commit v1 on v0

v1 whole, which is shorter than its diff:
```python
import math

import jax
import jax.numpy as jnp
import numpy as np
from jax import lax
from jax.experimental import pallas as pl
from jax.experimental.pallas import tpu as pltpu
from jax.sharding import PartitionSpec as P

MESH = pl.DeviceIdType.MESH
F32 = jnp.float32
BF16 = jnp.bfloat16


def angle_parts():
    lag = np.arange(1024, dtype=np.int64) - 512
    coarse = (np.arange(64, dtype=np.int64)[:, None] * 16 * lag[None]) % 2048
    fine = (np.arange(16, dtype=np.int64)[:, None] * lag[None]) % 2048
    scale = 1.0 / math.sqrt(8192.0)
    coarse = coarse * (math.pi / 1024)
    fine = fine * (math.pi / 1024)
    top = np.concatenate([np.cos(coarse), -np.sin(coarse)]) * scale
    low = np.concatenate([np.cos(fine), -np.sin(fine)])
    return top.astype(np.float32), low.astype(np.float32)


def place():
    blk = lax.axis_index("blk")
    lay = lax.axis_index("lay")
    x = lax.rem(lay, 4)
    y = lax.div(blk, 16)
    z = lax.div(lay, 4) * 8 + lax.div(lax.rem(blk, 16), 2)
    c = lax.rem(blk, 2)
    return blk, lay, x, y, z, c


def kernel(
    starts, ends, slots, spec_hbm, model_hbm, top_hbm, low_hbm, out,
    spec, model, top, low, raw, own_rows, ordered, partner, cross, left, table,
    model_rows, misfit, resp, own, part, outbox, inbox,
    load_sem, go_sem, come_sem, send_sem, recv_sem,
):
    blk, lay, x, y, z, c = place()
    loads = [
        pltpu.make_async_copy(spec_hbm, spec, load_sem.at[0]),
        pltpu.make_async_copy(top_hbm, top, load_sem.at[1]),
        pltpu.make_async_copy(low_hbm, low, load_sem.at[2]),
        pltpu.make_async_copy(model_hbm, model, load_sem.at[3]),
    ]
    for load in loads:
        load.start()
    loads[0].wait()
    for n in range(8):
        value = spec[n // 4, n % 4].astype(F32)
        for k in range(8):
            raw[pl.ds(n * 32 + k, 4, stride=8), :] = value[:, k * 128 : (k + 1) * 128]
    slot_of = [jnp.full((8, 128), slots[0, r], jnp.int32) for r in range(4)]
    chosen = [[slot_of[r] == q for q in range(4)] for r in range(4)]
    for n in range(8):
        for w in range(4):
            value = jnp.zeros((8, 128), F32)
            for q in range(4):
                at = ((n // 4) * 4 + q) * 32 + w * 8
                value = jnp.where(chosen[n % 4][q], raw[at : at + 8, :], value)
            own_rows[n * 32 + w * 8 : n * 32 + w * 8 + 8, :] = value
        ordered[n * 32 : (n + 1) * 32, :] = own_rows[n * 32 : (n + 1) * 32, :].astype(BF16)

    def forward(s):
        c2 = lax.rem(c + s, 2)
        far = 2 * x + lax.div(c2 + s, 2)
        z2 = lax.rem(z - far + 8 * lax.div(far + 3, 8) + 16, 16)
        y2 = lax.rem(y - lax.div(2 * z2 + c2 + 4 * x + s, 16) + 4, 4)
        return pltpu.make_async_remote_copy(
            src_ref=ordered,
            dst_ref=partner.at[s],
            send_sem=go_sem.at[s],
            recv_sem=come_sem.at[s],
            device_id=(
                y2 * 16 + lax.rem(z2, 8) * 2 + c2,
                lax.div(z2, 8) * 4 + x,
            ),
            device_id_type=MESH,
        )

    home = lay == 0

    @pl.when(home)
    def _():
        pltpu.make_async_copy(ordered, partner.at[0], come_sem.at[0]).start()

    @pl.when(jnp.logical_not(home))
    def _():
        forward(0).start()

    for s in range(1, 4):
        forward(s).start()

    loads[1].wait()
    loads[2].wait()

    @pl.loop(0, 64)
    def _(n):
        for q in range(4):
            at = slice(q * 256, (q + 1) * 256)
            cos_top = top[pl.ds(n, 1), at]
            sin_top = top[pl.ds(64 + n, 1), at]
            cos_low = low[0:16, at]
            sin_low = low[16:32, at]
            rows = pl.multiple_of(n * 16, 16)
            table[pl.ds(rows, 16), at] = (cos_top * cos_low - sin_top * sin_low).astype(BF16)
            table[pl.ds(1024 + rows, 16), at] = (sin_top * cos_low + cos_top * sin_low).astype(BF16)

    loads[3].wait()
    for n in range(16):
        model_rows[n * 4 : (n + 1) * 4, :] = model[0, n // 4, n % 4].astype(F32)

    @pl.when(home)
    def _():
        pltpu.make_async_copy(ordered, partner.at[0], come_sem.at[0]).wait()

    @pl.when(jnp.logical_not(home))
    def _():
        forward(0).wait()

    for s in range(1, 4):
        forward(s).wait()

    @pl.loop(0, 4)
    def _(s):
        re = [None] * 16
        im = [None] * 16
        for half in range(2):
            second = [
                partner[s, pl.ds(n * 32 + half * 16, 16), :].astype(F32) for n in range(8)
            ]
            for low_w in range(2):
                w = half * 2 + low_w
                first = [own_rows[n * 32 + w * 8 : n * 32 + w * 8 + 8, :] for n in range(8)]
                for i in range(4):
                    for j in range(4):
                        v_re = second[j][low_w * 8 : low_w * 8 + 8]
                        v_im = second[4 + j][low_w * 8 : low_w * 8 + 8]
                        a = first[i] * v_re + first[4 + i] * v_im
                        b = first[4 + i] * v_re - first[i] * v_im
                        n = i * 4 + j
                        re[n] = a if re[n] is None else re[n] + a
                        im[n] = b if im[n] is None else im[n] + b
        for n in range(16):
            at = pl.multiple_of(s * 128 + n * 8, 8)
            cross[pl.ds(at, 8), :] = re[n]
            cross[pl.ds(512 + at, 8), :] = im[n]

    for h in range(2):
        for k in range(8):
            left[:, h * 1024 + k * 128 : h * 1024 + (k + 1) * 128] = cross[
                pl.ds(h * 512 + k, 64, stride=8), :
            ].astype(BF16)

    row = lax.broadcasted_iota(jnp.int32, (64, 1), 0)
    offset = lax.div(row, 16)
    start = jnp.zeros((64, 1), jnp.int32)
    end = jnp.zeros((64, 1), jnp.int32)
    for s in range(4):
        start = jnp.where(offset == s, starts[0, s], start)
        end = jnp.where(offset == s, ends[0, s], end)
    diagonal = (lax.rem(lax.div(row, 4), 4) == lax.rem(row, 4)) & (offset == 0) & (lay == 0)
    end = jnp.where(diagonal, 0, end)

    @pl.loop(0, 4)
    def _(q):
        at = pl.multiple_of(q * 256, 256)
        lagged = jnp.dot(left[...], table[:, pl.ds(at, 256)], preferred_element_type=F32)
        lag = at + lax.broadcasted_iota(jnp.int32, (64, 256), 1)
        keep = (lag >= start) & (lag < end)
        misfit[:, pl.ds(at, 256)] = jnp.where(
            keep, lagged - model_rows[:, pl.ds(at, 256)], 0.0
        ).astype(BF16)

    @pl.loop(0, 8)
    def _(q):
        at = pl.multiple_of(q * 256, 256)
        value = lax.dot_general(
            misfit[...],
            table[pl.ds(at, 256), :],
            (((1,), (1,)), ((), ())),
            preferred_element_type=F32,
        )
        value = value.astype(BF16).astype(F32)
        base = lax.div(q, 4) * 512 + lax.rem(q, 4) * 2
        for k in range(2):
            resp[pl.ds(base + k, 64, stride=8), :] = value[:, k * 128 : (k + 1) * 128]

    @pl.loop(0, 4)
    def _(w):
        w8 = pl.multiple_of(w * 8, 8)
        w16 = pl.multiple_of(lax.div(w, 2) * 16, 16)
        odd = lax.rem(w, 2) == 1
        first = [own_rows[pl.ds(n * 32 + w8, 8), :] for n in range(8)]
        total = [jnp.zeros((8, 128), F32)] * 8
        for s in range(4):
            for j in range(4):
                pair_re = partner[s, pl.ds(j * 32 + w16, 16), :].astype(F32)
                pair_im = partner[s, pl.ds((4 + j) * 32 + w16, 16), :].astype(F32)
                v_re = jnp.where(odd, pair_re[8:], pair_re[:8])
                v_im = jnp.where(odd, pair_im[8:], pair_im[:8])
                part_re = jnp.zeros((8, 128), F32)
                part_im = jnp.zeros((8, 128), F32)
                for i in range(4):
                    at = (s * 16 + i * 4 + j) * 8
                    a = resp[at : at + 8, :]
                    b = resp[512 + at : 512 + at + 8, :]
                    total[i] = total[i] + (a * v_re - b * v_im)
                    total[4 + i] = total[4 + i] + (a * v_im + b * v_re)
                    part_re = part_re + (a * first[i] + b * first[4 + i])
                    part_im = part_im + (a * first[4 + i] - b * first[i])
                part[s, pl.ds(j * 32 + w8, 8), :] = part_re
                part[s, pl.ds((4 + j) * 32 + w8, 8), :] = part_im
        for n in range(8):
            own[pl.ds(n * 32 + w8, 8), :] = total[n]

    for k in range(8):
        outbox[32 + k] = own[pl.ds(k, 32, stride=8), :].astype(BF16)
        for s in range(4):
            outbox[k * 4 + s] = part[s, pl.ds(k, 32, stride=8), :].astype(BF16)

    def sends(n):
        s = lax.rem(n, 4)
        is_own = n >= 32
        to_lay = jnp.where(is_own, n - 32, lax.div(n, 4))
        to_blk = jnp.where(is_own, blk, lax.rem(blk + 4 * lay + s, 64))
        slot = jnp.where(is_own, 32 + lay, 4 * lay + s)
        return to_blk, to_lay, slot

    @pl.loop(0, 40)
    def _(n):
        to_blk, to_lay, slot = sends(n)
        here = (to_blk == blk) & (to_lay == lay)

        @pl.when(here)
        def _():
            pltpu.make_async_copy(outbox.at[n], inbox.at[slot], recv_sem).start()

        @pl.when(jnp.logical_not(here))
        def _():
            pltpu.make_async_remote_copy(
                src_ref=outbox.at[n],
                dst_ref=inbox.at[slot],
                send_sem=send_sem,
                recv_sem=recv_sem,
                device_id=(to_blk, to_lay),
                device_id_type=MESH,
            ).start()

    pltpu.make_async_copy(inbox, inbox, recv_sem).wait()

    @pl.when(home)
    def _():
        pltpu.make_async_copy(outbox.at[0:38], outbox.at[0:38], send_sem).wait()

    @pl.when(jnp.logical_not(home))
    def _():
        pltpu.make_async_copy(outbox.at[0:39], outbox.at[0:39], send_sem).wait()

    result = inbox[0].astype(F32)
    for n in range(1, 40):
        result = result + inbox[n].astype(F32)
    result = result * (1.0 / 16.0)
    raw[0:32, :] = result
    for p in range(2):
        for q in range(4):
            value = jnp.zeros((4, 128), F32)
            for r in range(4):
                at = p * 16 + r * 4
                value = jnp.where(chosen[r][q][:4], raw[at : at + 4, :], value)
            out[p, q] = value


def local(spectra, model_corr, window_start, window_end, station_slot):
    top, low = angle_parts()
    smem = pl.BlockSpec(memory_space=pltpu.SMEM)
    hbm = pl.BlockSpec(memory_space=pl.ANY)
    return pl.pallas_call(
        kernel,
        out_shape=jax.ShapeDtypeStruct((2, 4, 4, 128), F32),
        in_specs=[smem] * 3 + [hbm] * 4,
        out_specs=pl.BlockSpec(memory_space=pltpu.VMEM),
        scratch_shapes=[
            pltpu.VMEM((2, 4, 4, 1024), BF16),
            pltpu.VMEM((1, 4, 4, 4, 1024), BF16),
            pltpu.VMEM((128, 1024), F32),
            pltpu.VMEM((32, 1024), F32),
            pltpu.VMEM((256, 128), F32),
            pltpu.VMEM((256, 128), F32),
            pltpu.VMEM((256, 128), BF16),
            pltpu.VMEM((4, 256, 128), BF16),
            pltpu.VMEM((1024, 128), F32),
            pltpu.VMEM((64, 2048), BF16),
            pltpu.VMEM((2048, 1024), BF16),
            pltpu.VMEM((64, 1024), F32),
            pltpu.VMEM((64, 1024), BF16),
            pltpu.VMEM((1024, 128), F32),
            pltpu.VMEM((256, 128), F32),
            pltpu.VMEM((4, 256, 128), F32),
            pltpu.VMEM((40, 32, 128), BF16),
            pltpu.VMEM((40, 32, 128), BF16),
            pltpu.SemaphoreType.DMA((4,)),
            pltpu.SemaphoreType.DMA((4,)),
            pltpu.SemaphoreType.DMA((4,)),
            pltpu.SemaphoreType.DMA,
            pltpu.SemaphoreType.DMA,
        ],
        compiler_params=pltpu.CompilerParams(has_side_effects=True),
        name="adjoint",
    )(
        window_start, window_end, station_slot, spectra, model_corr,
        jnp.asarray(top), jnp.asarray(low),
    )


def solution(mesh):
    in_specs = (
        P(None, "blk", None, None),
        P("blk", "lay", None, None, None),
        P("blk", "lay"),
        P("blk", "lay"),
        P("blk", None),
    )
    out_specs = P(None, "blk", None, "lay")
    return jax.shard_map(local, mesh=mesh, in_specs=in_specs, out_specs=out_specs, check_vma=False)
```

time: 325 us -> 75.6 us (0.23)
  the two profiles are of different devices: /device:TPU:1 before, /device:TPU:39 now
where the time goes in v1:
time: 75.6 us; the launch traced here: 75.4 us
  Pallas kernels  74.1 us (98%)
  local copies, waits for them, and re-layouts  1.32 us (2%)
    pallas_call x1, Pallas kernels, local(): pl.pallas_call(kernel, out_shape=jax.ShapeDtypeStruct((2, 4, 4, 128), F32...  74.1 us

profile of v1, /device:TPU:39, one launch (start us, length us, event | category | flops | bytes accessed | tf_op | source)
XLA Modules:
  0.0 75.4 jit_solution(17760704993205543459)
XLA Ops:
  0.0 74.1 %adjoint.1 = f32[2,4,4,128]{3,2,1,0:T(4,128)} custom-call(s32[1,4]{1,0:T(1,128)} %starts.1, s32[1,4]{1,0:T(1,128)} %ends.1, s32[1,4]{1,0:T(1,128)} %slots.1, bf16[2,4,4,1024]{3,2,1,0:T(4,128)(2,1)} %spec_hbm.1, bf16[1,4,4,4,1024]{4,3,2,1,0:T(4,128)(2,1)} %model_hbm.1, f32[128,1024]{1,0:T(8,128)} %constant.4.clone.top_hbm, f32[32,1024]{1,0:T(8,128)} %constant.5.clone.low_hbm), custom_call_target="tpu_custom_call" | custom-call | tf_op jit(solution)/shard_map/adjoint/pallas_call | solution.py:283
  74.1 1.3 %copy.9 = f32[2,4,4,128]{3,2,1,0:T(4,128)} copy(f32[2,4,4,128]{3,2,1,0:T(4,128)} %adjoint.1) | data formatting | bytes 32768

commit v2 on v0

v2 whole, which is shorter than its diff:
```python
import math

import jax
import jax.numpy as jnp
import numpy as np
from jax import lax
from jax.experimental import pallas as pl
from jax.experimental.pallas import tpu as pltpu
from jax.sharding import PartitionSpec as P

MESH = pl.DeviceIdType.MESH
F32 = jnp.float32
BF16 = jnp.bfloat16

SOURCE = [[3, 1, 0, 0, 0], [2, 0, 1, 1, 1], [3, 2, 2, 2, 1], [3, 3, 0, 3, 2]]
AHEAD = [[0, 0, 1, 1, 2], [2, 2, 3, 3, -4], [4, 4, -3, -3, -2], [-2, -2, -1, -1, 0]]
SENT = [
    [[(x, q) for x in range(4) for q in range(core, 5, 2) if SOURCE[x][q] == source] for core in range(2)]
    for source in range(4)
]


def angle_parts():
    lag = np.arange(1024, dtype=np.int64) - 512
    coarse = (np.arange(64, dtype=np.int64)[:, None] * 16 * lag[None]) % 2048
    fine = (np.arange(16, dtype=np.int64)[:, None] * lag[None]) % 2048
    scale = 1.0 / math.sqrt(8192.0)
    coarse = coarse * (math.pi / 1024)
    fine = fine * (math.pi / 1024)
    top = np.concatenate([np.cos(coarse), -np.sin(coarse)]) * scale
    low = np.concatenate([np.cos(fine), -np.sin(fine)])
    return top.astype(np.float32), low.astype(np.float32)


def choose(index, values):
    result = jnp.int32(values[0])
    for n in range(1, len(values)):
        result = jnp.where(index == n, jnp.int32(values[n]), result)
    return result


def kernel(
    starts, ends, slots, spec_hbm, model_hbm, top_hbm, low_hbm, out,
    spec, model, top, low, raw, halves, ordered, peer_half, first, partner, cross, left, left_out,
    table, model_rows, lagged, misfit, resp, resp_out, resp_rows, own, part, outbox, inbox, merged, last,
    load_sem, peer_send, peer_recv, go_sem, come_sem, x_send, x_recv, z_send, z_recv,
):
    blk = lax.axis_index("blk")
    lay = lax.axis_index("lay")
    x = lax.rem(lay, 4)
    y = lax.div(blk, 16)
    zl = lax.div(lax.rem(blk, 16), 2)
    zh = lax.div(lay, 4)
    z = zh * 8 + zl
    c = lax.rem(blk, 2)
    other = 1 - c

    def device(x1, y1, z1, c1):
        return lax.rem(y1 + 8, 4) * 16 + lax.rem(z1, 8) * 2 + c1, lax.div(z1, 8) * 4 + x1

    peer = device(x, y, z, other)

    def receiver(n, core):
        to_x = jnp.where(
            c == 0,
            choose(x, [SENT[s][0][n][0] for s in range(4)]),
            choose(x, [SENT[s][1][min(n, 1)][0] for s in range(4)]),
        )
        q = jnp.where(
            c == 0,
            choose(x, [SENT[s][0][n][1] for s in range(4)]),
            choose(x, [SENT[s][1][min(n, 1)][1] for s in range(4)]),
        )
        ahead = jnp.where(
            c == 0,
            choose(x, [AHEAD[a][b] for a, b in (SENT[s][0][n] for s in range(4))]),
            choose(x, [AHEAD[a][b] for a, b in (SENT[s][1][min(n, 1)] for s in range(4))]),
        )
        to_z = lax.rem(z - ahead + 16, 16)
        to_y = y - lax.div(to_z + 2 * to_x + lax.div(q, 2), 8)
        return device(to_x, to_y, to_z, core), q

    def sender(q):
        from_z = lax.rem(z + choose(x, [AHEAD[s][q] for s in range(4)]) + 16, 16)
        from_y = y + lax.div(z + 2 * x + q // 2, 8)
        return device(choose(x, [SOURCE[s][q] for s in range(4)]), from_y, from_z, q % 2)

    def target(m):
        to_blk = 16 * y + 2 * zl + m - 17 if m >= 17 else lax.rem(16 * y + 2 * z + m, 64)
        slot = 16 + zh if m >= 17 else (m // 2) * 2 + zh + (2 if m == 16 else 0)
        return (to_blk, c * 4 + x), slot

    def elsewhere(to):
        return (to[0] != blk) | (to[1] != lay)

    barrier = pltpu.get_barrier_semaphore()

    def greet(to):
        pl.semaphore_signal(barrier, inc=1, device_id=to, device_id_type=MESH)

    for q in range(5):
        greet(sender(q))
    greet(peer)
    for t in range(1, 4):
        greet((blk, zh * 4 + lax.rem(x + t, 4)))
    for half in range(2):
        to = (16 * y + 2 * zl + zh, half * 4 + x)

        @pl.when(elsewhere(to))
        def _():
            greet(to)

        @pl.loop(0, 9 - c)
        def _(j):
            from_zl = lax.rem(zl - j + 8, 8)
            from_y = y - half + lax.div(zl - j + 8, 8) - 1
            to = device(x, from_y, half * 8 + from_zl, zh)

            @pl.when(elsewhere(to))
            def _():
                greet(to)

    loads = [
        pltpu.make_async_copy(spec_hbm, spec, load_sem.at[0]),
        pltpu.make_async_copy(top_hbm, top, load_sem.at[1]),
        pltpu.make_async_copy(low_hbm, low, load_sem.at[2]),
        pltpu.make_async_copy(model_hbm, model, load_sem.at[3]),
    ]
    for load in loads:
        load.start()
    with jax.named_scope("p01order"):
        loads[0].wait()
        for n in range(8):
            value = spec[n // 4, n % 4].astype(F32)
            for k in range(8):
                raw[pl.ds(n * 32 + k, 4, stride=8), :] = value[:, k * 128 : (k + 1) * 128]
        slot_of = [jnp.full((8, 128), slots[0, r], jnp.int32) for r in range(4)]
        chosen = [[slot_of[r] == q for q in range(4)] for r in range(4)]
        for p in range(2):
            for r in range(4):
                for w in range(4):
                    value = jnp.zeros((8, 128), F32)
                    for q in range(4):
                        at = (p * 4 + q) * 32 + w * 8
                        value = jnp.where(chosen[r][q], raw[at : at + 8, :], value)
                    at = ((p * 4 + w) * 4 + r) * 4
                    halves[0, at : at + 4, :] = value[:4]
                    halves[1, at : at + 4, :] = value[4:]
        for h in range(2):
            ordered[h] = halves[h].astype(BF16)

    with jax.named_scope("p02barrier"):
        mine = jnp.where(c == zh, 1, 0) + jnp.where((c == 0) & (zh == 0), 1, 0)
        pl.semaphore_wait(barrier, 23 + 6 - 2 * c - mine)

    peer_copy = pltpu.make_async_remote_copy(
        src_ref=ordered.at[other],
        dst_ref=peer_half,
        send_sem=peer_send.at[0],
        recv_sem=peer_recv.at[0],
        device_id=peer,
        device_id_type=MESH,
    )

    def forward(n, core):
        to, q = receiver(n, core)
        return pltpu.make_async_remote_copy(
            src_ref=ordered.at[core],
            dst_ref=partner.at[q],
            send_sem=go_sem.at[2 * n + core],
            recv_sem=come_sem.at[q],
            device_id=to,
            device_id_type=MESH,
        )

    with jax.named_scope("p03fwd"):
        for n in range(2):
            for core in range(2):
                forward(n, core).start()

        @pl.when(c == 0)
        def _():
            for core in range(2):
                forward(2, core).start()

        peer_copy.start()

    with jax.named_scope("p04table"):
        loads[1].wait()
        loads[2].wait()

        @pl.loop(0, 64)
        def _(n):
            h = lax.div(n, 32)
            at_row = pl.multiple_of(lax.rem(n, 32) * 16, 16)
            for q in range(4):
                at = slice(q * 256, (q + 1) * 256)
                cos_top = top[pl.ds(n, 1), at]
                sin_top = top[pl.ds(64 + n, 1), at]
                cos_low = low[0:16, at]
                sin_low = low[16:32, at]
                table[h, pl.ds(at_row, 16), at] = (cos_top * cos_low - sin_top * sin_low).astype(BF16)
                table[h, pl.ds(512 + at_row, 16), at] = (sin_top * cos_low + cos_top * sin_low).astype(BF16)

        loads[3].wait()
        for n in range(16):
            model_rows[n * 4 : (n + 1) * 4, :] = model[0, n // 4, n % 4].astype(F32)

        peer_copy.wait()
        for t in range(2):
            source = jnp.where(t == c, halves[c], peer_half[...].astype(F32))
            raw[0:128, :] = source
            for n in range(32):
                value = raw[n * 4 : n * 4 + 4, :]
                first[t, n * 8 : n * 8 + 4, :] = value
                first[t, n * 8 + 4 : n * 8 + 8, :] = value

    with jax.named_scope("p05fwdwait"):
        for q in range(5):
            pltpu.make_async_copy(partner.at[q], partner.at[q], come_sem.at[q]).wait()

    def cross_of(t):
        @pl.loop(0, 4)
        def _(s):
            re = [None] * 8
            im = [None] * 8
            for w in range(4):
                u = [
                    first[t, ((p * 4 + w) * 4 + i) * 8 : ((p * 4 + w) * 4 + i) * 8 + 8, :]
                    for p in range(2)
                    for i in range(4)
                ]
                v_re = partner[t + s, w * 16 : w * 16 + 16, :].astype(F32)
                v_im = partner[t + s, 64 + w * 16 : 64 + w * 16 + 16, :].astype(F32)
                for i in range(4):
                    for jp in range(2):
                        a_re = v_re[jp * 8 : jp * 8 + 8]
                        a_im = v_im[jp * 8 : jp * 8 + 8]
                        a = u[i] * a_re + u[4 + i] * a_im
                        b = u[4 + i] * a_re - u[i] * a_im
                        n = i * 2 + jp
                        re[n] = a if w == 0 else re[n] + a
                        im[n] = b if w == 0 else im[n] + b
            for n in range(8):
                at = pl.multiple_of(s * 64 + n * 8, 8)
                cross[pl.ds(at, 8), :] = re[n]
                cross[pl.ds(256 + at, 8), :] = im[n]

    def gather(into):
        for h in range(2):
            for k in range(4):
                into[:, h * 512 + k * 128 : h * 512 + (k + 1) * 128] = cross[
                    pl.ds(h * 256 + k, 64, stride=4), :
                ].astype(BF16)

    left_copy = pltpu.make_async_remote_copy(
        src_ref=left_out,
        dst_ref=left.at[1],
        send_sem=peer_send.at[1],
        recv_sem=peer_recv.at[1],
        device_id=peer,
        device_id_type=MESH,
    )
    with jax.named_scope("p06cross"):
        cross_of(other)
        gather(left_out)
        left_copy.start()
        cross_of(c)
        gather(left.at[0])

    with jax.named_scope("p07lag"):
        @pl.loop(0, 4)
        def _(q):
            at = pl.multiple_of(q * 256, 256)
            lagged[:, pl.ds(at, 256)] = jnp.dot(
                left[0], table[c, :, pl.ds(at, 256)], preferred_element_type=F32
            )

        row = lax.broadcasted_iota(jnp.int32, (64, 1), 0)
        offset = lax.div(row, 16)
        start = jnp.zeros((64, 1), jnp.int32)
        end = jnp.zeros((64, 1), jnp.int32)
        for s in range(4):
            start = jnp.where(offset == s, starts[0, s], start)
            end = jnp.where(offset == s, ends[0, s], end)
        diagonal = (lax.rem(lax.div(row, 4), 4) == lax.rem(row, 4)) & (offset == 0) & (lay == 0)
        end = jnp.where(diagonal, 0, end)
        left_copy.wait()

        @pl.loop(0, 4)
        def _(q):
            at = pl.multiple_of(q * 256, 256)
            value = lagged[:, pl.ds(at, 256)] + jnp.dot(
                left[1], table[other, :, pl.ds(at, 256)], preferred_element_type=F32
            )
            lag = at + lax.broadcasted_iota(jnp.int32, (64, 256), 1)
            keep = (lag >= start) & (lag < end)
            misfit[:, pl.ds(at, 256)] = jnp.where(
                keep, value - model_rows[:, pl.ds(at, 256)], 0.0
            ).astype(BF16)

    resp_copy = pltpu.make_async_remote_copy(
        src_ref=resp_out,
        dst_ref=resp.at[1],
        send_sem=peer_send.at[2],
        recv_sem=peer_recv.at[2],
        device_id=peer,
        device_id_type=MESH,
    )

    def respond(h, into):
        @pl.loop(0, 4)
        def _(q):
            at = pl.multiple_of(q * 256, 256)
            into[:, pl.ds(at, 256)] = lax.dot_general(
                misfit[...],
                table[h, pl.ds(at, 256), :],
                (((1,), (1,)), ((), ())),
                preferred_element_type=F32,
            ).astype(BF16)

    def spread(n, t):
        for p in range(2):
            for k in range(4):
                resp_rows[t, pl.ds(p * 256 + k, 64, stride=4), :] = resp[
                    n, :, p * 512 + k * 128 : p * 512 + (k + 1) * 128
                ].astype(F32)

    with jax.named_scope("p08resp"):
        respond(other, resp_out)
        resp_copy.start()
        respond(c, resp.at[0])
        spread(0, c)
        resp_copy.wait()
        spread(1, other)

    with jax.named_scope("p09terms"):

        @pl.loop(0, 4)
        def _(w):
            at_u = [pl.multiple_of(((p * 4 + w) * 4) * 8, 8) for p in range(2)]
            at_v = [pl.multiple_of((p * 4 + w) * 16, 16) for p in range(2)]
            u = [
                [first[t, pl.ds(at_u[p] + i * 8, 8), :] for p in range(2) for i in range(4)]
                for t in range(2)
            ]
            total = [[jnp.zeros((8, 128), F32)] * 8 for t in range(2)]
            for q in range(5):
                v = [partner[q, pl.ds(at_v[p], 16), :].astype(F32) for p in range(2)]
                for jp in range(2):
                    v_re = v[0][jp * 8 : jp * 8 + 8]
                    v_im = v[1][jp * 8 : jp * 8 + 8]
                    part_re = jnp.zeros((8, 128), F32)
                    part_im = jnp.zeros((8, 128), F32)
                    for t in range(2):
                        s = q - t
                        if not 0 <= s < 4:
                            continue
                        for i in range(4):
                            at = ((s * 4 + i) * 2 + jp) * 8
                            a = resp_rows[t, at : at + 8, :]
                            b = resp_rows[t, 256 + at : 256 + at + 8, :]
                            total[t][i] = total[t][i] + (a * v_re - b * v_im)
                            total[t][4 + i] = total[t][4 + i] + (a * v_im + b * v_re)
                            part_re = part_re + (a * u[t][i] + b * u[t][4 + i])
                            part_im = part_im + (a * u[t][4 + i] - b * u[t][i])
                    part[q, pl.ds(at_v[0] + jp * 8, 8), :] = part_re
                    part[q, pl.ds(at_v[1] + jp * 8, 8), :] = part_im
            for t in range(2):
                for p in range(2):
                    for i in range(4):
                        own[t, pl.ds(((p * 4 + i) * 4 + w) * 8, 8), :] = total[t][p * 4 + i]

    with jax.named_scope("p10pack"):
        for k in range(4):
            for t in range(2):
                outbox[k, 5 + t] = (
                    own[t, pl.ds(k, 32, stride=8), :] + own[t, pl.ds(4 + k, 32, stride=8), :]
                ).astype(BF16)
            for q in range(5):
                outbox[k, q] = part[q, pl.ds(k, 32, stride=4), :].astype(BF16)

    def across(t):
        to = lax.rem(x + t, 4)
        return pltpu.make_async_remote_copy(
            src_ref=outbox.at[to],
            dst_ref=inbox.at[x],
            send_sem=x_send.at[t - 1],
            recv_sem=x_recv.at[x],
            device_id=(blk, zh * 4 + to),
            device_id_type=MESH,
        )

    def deliver(source, m):
        to, slot = target(m)

        def start():
            pltpu.make_async_remote_copy(
                src_ref=source,
                dst_ref=last.at[slot],
                send_sem=z_send,
                recv_sem=z_recv,
                device_id=to,
                device_id_type=MESH,
            ).start()

        if m in (0, 17, 18):
            away = elsewhere(to)
            pl.when(away)(start)

            @pl.when(jnp.logical_not(away))
            def _():
                pltpu.make_async_copy(source, last.at[slot], z_recv).start()
        else:
            start()

    with jax.named_scope("p11x"):
        for t in (2, 1, 3):
            across(t).start()
        keep_copy = pltpu.make_async_copy(outbox.at[x], inbox.at[x], x_recv.at[x])
        keep_copy.start()
        for n in range(4):
            pltpu.make_async_copy(inbox.at[n], inbox.at[n], x_recv.at[n]).wait()

    with jax.named_scope("p12merge"):
        for n in range(4):
            for r in range(1, 4):
                deliver(inbox.at[n, r], 4 * n + r)
        deliver(inbox.at[0, 0], 0)
        deliver(inbox.at[3, 4], 16)
        for t in range(2):
            value = inbox[0, 5 + t].astype(F32)
            for n in range(1, 4):
                value = value + inbox[n, 5 + t].astype(F32)
            merged[3 + t] = value.astype(BF16)
        for n in range(1, 4):
            merged[n - 1] = (inbox[n, 0].astype(F32) + inbox[n - 1, 4].astype(F32)).astype(BF16)
        for n in range(1, 4):
            deliver(merged.at[n - 1], 4 * n)
        for t in range(2):
            deliver(merged.at[3 + t], 17 + t)

    with jax.named_scope("p13wait"):

        @pl.when(c == 0)
        def _():
            pltpu.make_async_copy(last, last, z_recv).wait()

        @pl.when(c == 1)
        def _():
            pltpu.make_async_copy(last.at[0:18], last.at[0:18], z_recv).wait()

    with jax.named_scope("p14sum"):
        total = last[0].astype(F32)
        for n in range(1, 16):
            total = total + last[n].astype(F32)
        scale = 1.0 / 16.0
        raw[32:64, :] = (last[16].astype(F32) + last[17].astype(F32)) * scale

        @pl.when(c == 0)
        def _():
            raw[0:32, :] = (total + last[18].astype(F32) + last[19].astype(F32)) * scale

        @pl.when(c == 1)
        def _():
            raw[0:32, :] = total * scale

        for p in range(2):
            row_of = [
                raw[pl.ds(p * 16 + r, 4, stride=4), :]
                + raw[32 + p * 16 + r * 4 : 32 + p * 16 + r * 4 + 4, :]
                for r in range(4)
            ]
            for q in range(4):
                value = jnp.zeros((4, 128), F32)
                for r in range(4):
                    value = jnp.where(chosen[r][q][:4], row_of[r], value)
                out[p, q] = value

        for n in range(2):
            for core in range(2):
                forward(n, core).wait_send()

        @pl.when(c == 0)
        def _():
            for core in range(2):
                forward(2, core).wait_send()

        for t in range(1, 4):
            across(t).wait_send()
        for n in range(3):

            @pl.when(mine == n)
            def _():
                gone = last.at[0 : 19 - n]
                pltpu.make_async_copy(gone, gone, z_send).wait()


def local(spectra, model_corr, window_start, window_end, station_slot):
    top, low = angle_parts()
    smem = pl.BlockSpec(memory_space=pltpu.SMEM)
    hbm = pl.BlockSpec(memory_space=pl.ANY)
    dma = pltpu.SemaphoreType.DMA
    return pl.pallas_call(
        kernel,
        out_shape=jax.ShapeDtypeStruct((2, 4, 4, 128), F32),
        in_specs=[smem] * 3 + [hbm] * 4,
        out_specs=pl.BlockSpec(memory_space=pltpu.VMEM),
        scratch_shapes=[
            pltpu.VMEM((2, 4, 4, 1024), BF16),
            pltpu.VMEM((1, 4, 4, 4, 1024), BF16),
            pltpu.VMEM((128, 1024), F32),
            pltpu.VMEM((32, 1024), F32),
            pltpu.VMEM((256, 128), F32),
            pltpu.VMEM((2, 128, 128), F32),
            pltpu.VMEM((2, 128, 128), BF16),
            pltpu.VMEM((128, 128), BF16),
            pltpu.VMEM((2, 256, 128), F32),
            pltpu.VMEM((5, 128, 128), BF16),
            pltpu.VMEM((512, 128), F32),
            pltpu.VMEM((2, 64, 1024), BF16),
            pltpu.VMEM((64, 1024), BF16),
            pltpu.VMEM((2, 1024, 1024), BF16),
            pltpu.VMEM((64, 1024), F32),
            pltpu.VMEM((64, 1024), F32),
            pltpu.VMEM((64, 1024), BF16),
            pltpu.VMEM((2, 64, 1024), BF16),
            pltpu.VMEM((64, 1024), BF16),
            pltpu.VMEM((2, 512, 128), F32),
            pltpu.VMEM((2, 256, 128), F32),
            pltpu.VMEM((5, 128, 128), F32),
            pltpu.VMEM((4, 7, 32, 128), BF16),
            pltpu.VMEM((4, 7, 32, 128), BF16),
            pltpu.VMEM((5, 32, 128), BF16),
            pltpu.VMEM((20, 32, 128), BF16),
            dma((4,)), dma((3,)), dma((3,)), dma((6,)), dma((5,)), dma((3,)), dma((4,)), dma, dma,
        ],
        compiler_params=pltpu.CompilerParams(has_side_effects=True, collective_id=0),
        name="adjoint",
    )(
        window_start, window_end, station_slot, spectra, model_corr,
        jnp.asarray(top), jnp.asarray(low),
    )


def solution(mesh):
    in_specs = (
        P(None, "blk", None, None),
        P("blk", "lay", None, None, None),
        P("blk", "lay"),
        P("blk", "lay"),
        P("blk", None),
    )
    out_specs = P(None, "blk", None, "lay")
    return jax.shard_map(local, mesh=mesh, in_specs=in_specs, out_specs=out_specs, check_vma=False)
```

time: 325 us -> 48 us (0.15)
  waiting for transfers between devices: 177 us -> 0 us
  starting transfers between devices: 93.9 us -> 0 us
  Pallas kernels: 0 us -> 46.1 us
  other arithmetic: 24.7 us -> 0 us
  between operations: 13.8 us -> 0.01 us
  local copies, waits for them, and re-layouts: 10 us -> 1.32 us
  matrix products: 3.99 us -> 0 us
    unnamed x2 -> x0, waiting for transfers between devices: 115 us -> none
    ppermute x13 -> x0, starting transfers between devices: 93.9 us -> none  [from_behind(): return lax.ppermute(value, axis, pairs)]
    ppermute x13 -> x0, waiting for transfers between devices: 62.8 us -> none  [from_behind(): return lax.ppermute(value, axis, pairs)]
    pallas_call x0 -> x1, Pallas kernels: none -> 46.1 us  [local(): pl.pallas_call(kernel, out_shape=jax.ShapeDtypeStruct((2, 4, 4, 128), F32...]
    convert_element_type x9 -> x0, other arithmetic: 20 us -> none  [the longest x1 18.2 us: lag_table(): cosine = (jnp.cos(angle) * factor).astype(jnp.bfloat16)]
    unnamed x12 -> x1, local copies, waits for them, and re-layouts: 9.52 us -> 1.32 us
    reduce_sum x4 -> x0, other arithmetic: 4.18 us -> none  [the longest x1 1.66 us: cross_of(): jnp.sum(first[0][:, None] * second[0][None] + first[1][:, None] * second[...]
    dot_general x2 -> x0, matrix products: 3.99 us -> none  [the longest x1 2.59 us: local(): jnp.dot(cross_all, table, preferred_element_type=jnp.float32)]
  transfers between devices with their start and end apart: 14 -> 0, of which waited for: 13 -> 0; matrix products, arithmetic and copies ran while one was open for 6% -> 0% of each run, Pallas kernels for 0% -> 0%
where the time goes in v2:
time: 48 us; the launch traced here: 47.5 us
  Pallas kernels  46.1 us (96%)
  local copies, waits for them, and re-layouts  1.32 us (3%)
    pallas_call x1, Pallas kernels, local(): pl.pallas_call(kernel, out_shape=jax.ShapeDtypeStruct((2, 4, 4, 128), F32...  46.1 us
    unnamed x1, local copies, waits for them, and re-layouts  1.32 us

profile of v2, /device:TPU:1, one launch (start us, length us, event | category | flops | bytes accessed | tf_op | source)
XLA Modules:
  0.0 47.5 jit_solution(1609128599722495555)
XLA Ops:
  0.0 46.1 %adjoint.1 = f32[2,4,4,128]{3,2,1,0:T(4,128)} custom-call(s32[1,4]{1,0:T(1,128)} %starts.1, s32[1,4]{1,0:T(1,128)} %ends.1, s32[1,4]{1,0:T(1,128)} %slots.1, bf16[2,4,4,1024]{3,2,1,0:T(4,128)(2,1)} %spec_hbm.1, bf16[1,4,4,4,1024]{4,3,2,1,0:T(4,128)(2,1)} %model_hbm.1, f32[128,1024]{1,0:T(8,128)} %constant.4.clone.top_hbm, f32[32,1024]{1,0:T(8,128)} %constant.5.clone.low_hbm), custom_call_target="tpu_custom_call" | custom-call | tf_op jit(solution)/shard_map/adjoint/pallas_call | solution.py:504
  46.1 1.3 %copy.9 = f32[2,4,4,128]{3,2,1,0:T(4,128)} copy(f32[2,4,4,128]{3,2,1,0:T(4,128)} %adjoint.1) | data formatting | bytes 32768

commit v3 on v2

--- a/solution.py
+++ b/solution.py
@@ -29,7 +29,15 @@
     fine = fine * (math.pi / 1024)
     top = np.concatenate([np.cos(coarse), -np.sin(coarse)]) * scale
     low = np.concatenate([np.cos(fine), -np.sin(fine)])
-    return top.astype(np.float32), low.astype(np.float32)
+    freq = np.arange(1024, dtype=np.int64)
+    coarse = ((np.arange(64, dtype=np.int64)[:, None] * 16 - 512) * freq[None]) % 2048
+    fine = (np.arange(16, dtype=np.int64)[:, None] * freq[None]) % 2048
+    coarse = coarse * (math.pi / 1024)
+    fine = fine * (math.pi / 1024)
+    top2 = np.concatenate([np.cos(coarse), -np.sin(coarse)]) * scale
+    low2 = np.concatenate([np.cos(fine), -np.sin(fine)])
+    both = np.stack([np.concatenate([top, low]), np.concatenate([top2, low2])])
+    return both.astype(np.float32)
 
 
 def choose(index, values):
@@ -40,10 +48,10 @@
 
 
 def kernel(
-    starts, ends, slots, spec_hbm, model_hbm, top_hbm, low_hbm, out,
-    spec, model, top, low, raw, halves, ordered, peer_half, first, partner, cross, left, left_out,
-    table, model_rows, lagged, misfit, resp, resp_out, resp_rows, own, part, outbox, inbox, merged, last,
-    load_sem, peer_send, peer_recv, go_sem, come_sem, x_send, x_recv, z_send, z_recv,
+    starts_hbm, ends_hbm, slots_hbm, spec_hbm, model_hbm, angles_hbm, out,
+    starts, ends, slots, spec, model, angles, raw, halves, ordered, peer_half, first, partner, cross, left, left_out,
+    table, turned, model_rows, lagged, misfit, resp, resp_out, resp_rows, own, part, outbox, inbox, merged, last,
+    load_sem, ring_sem, peer_send, peer_recv, go_sem, come_sem, x_send, x_recv, z_send, z_recv,
 ):
     blk = lax.axis_index("blk")
     lay = lax.axis_index("lay")
@@ -85,13 +93,27 @@
         from_y = y + lax.div(z + 2 * x + q // 2, 8)
         return device(choose(x, [SOURCE[s][q] for s in range(4)]), from_y, from_z, q % 2)
 
+    mine = jnp.where(c == zh, 1, 0) + jnp.where((c == 0) & (zh == 0), 1, 0)
+
     def target(m):
-        to_blk = 16 * y + 2 * zl + m - 17 if m >= 17 else lax.rem(16 * y + 2 * z + m, 64)
-        slot = 16 + zh if m >= 17 else (m // 2) * 2 + zh + (2 if m == 16 else 0)
-        return (to_blk, c * 4 + x), slot
+        if isinstance(m, int) and m >= 17:
+            return (16 * y + 2 * zl + m - 17, c * 4 + x), 16 + zh
+        slot = lax.div(m, 2) * 2 + zh + (2 if isinstance(m, int) and m == 16 else 0)
+        return (lax.rem(16 * y + 2 * z + m, 64), c * 4 + x), slot
 
     def elsewhere(to):
         return (to[0] != blk) | (to[1] != lay)
+
+    loads = [
+        pltpu.make_async_copy(spec_hbm, spec, load_sem.at[0]),
+        pltpu.make_async_copy(slots_hbm, slots, load_sem.at[1]),
+        pltpu.make_async_copy(angles_hbm, angles, load_sem.at[2]),
+        pltpu.make_async_copy(model_hbm, model, load_sem.at[3]),
+        pltpu.make_async_copy(starts_hbm, starts, load_sem.at[4]),
+        pltpu.make_async_copy(ends_hbm, ends, load_sem.at[5]),
+    ]
+    for load in loads:
+        load.start()
 
     barrier = pltpu.get_barrier_semaphore()
 
@@ -103,33 +125,27 @@
     greet(peer)
     for t in range(1, 4):
         greet((blk, zh * 4 + lax.rem(x + t, 4)))
-    for half in range(2):
-        to = (16 * y + 2 * zl + zh, half * 4 + x)
-
-        @pl.when(elsewhere(to))
-        def _():
+    near = [
+        [device(x, y + d, z, c) for d in (-1, 1)],
+        [device(x, y, lax.rem(z + d + 16, 16), c) for d in (-1, 1)],
+        [device(x, y, lax.rem(z + d + 16, 16), c) for d in (-2, 2)],
+        [device(x, y, lax.rem(z + d + 16, 16), c) for d in (-4, 4)],
+        [device(x, y + d, z, c) for d in (-1, 1)],
+    ]
+    for pair in near[:2]:
+        for to in pair:
             greet(to)
 
-        @pl.loop(0, 9 - c)
-        def _(j):
-            from_zl = lax.rem(zl - j + 8, 8)
-            from_y = y - half + lax.div(zl - j + 8, 8) - 1
-            to = device(x, from_y, half * 8 + from_zl, zh)
-
-            @pl.when(elsewhere(to))
-            def _():
-                greet(to)
-
-    loads = [
-        pltpu.make_async_copy(spec_hbm, spec, load_sem.at[0]),
-        pltpu.make_async_copy(top_hbm, top, load_sem.at[1]),
-        pltpu.make_async_copy(low_hbm, low, load_sem.at[2]),
-        pltpu.make_async_copy(model_hbm, model, load_sem.at[3]),
-    ]
-    for load in loads:
-        load.start()
+    def tell(n):
+        for to in near[n]:
+            pl.semaphore_signal(ring_sem.at[n], inc=1, device_id=to, device_id_type=MESH)
+
+    def told(n):
+        pl.semaphore_wait(ring_sem.at[n], 2)
+
     with jax.named_scope("p01order"):
         loads[0].wait()
+        loads[1].wait()
         for n in range(8):
             value = spec[n // 4, n % 4].astype(F32)
             for k in range(8):
@@ -149,9 +165,25 @@
         for h in range(2):
             ordered[h] = halves[h].astype(BF16)
 
+    with jax.named_scope("p01table"):
+        loads[2].wait()
+
+        @pl.loop(0, 64)
+        def _(n):
+            h = lax.div(n, 32)
+            at_row = pl.multiple_of(lax.rem(n, 32) * 16, 16)
+            for q in range(4):
+                at = slice(q * 256, (q + 1) * 256)
+                cos_top = angles[0, pl.ds(n, 1), at]
+                sin_top = angles[0, pl.ds(64 + n, 1), at]
+                cos_low = angles[0, 128:144, at]
+                sin_low = angles[0, 144:160, at]
+                table[h, pl.ds(at_row, 16), at] = (cos_top * cos_low - sin_top * sin_low).astype(BF16)
+                table[h, pl.ds(512 + at_row, 16), at] = (sin_top * cos_low + cos_top * sin_low).astype(BF16)
+
     with jax.named_scope("p02barrier"):
-        mine = jnp.where(c == zh, 1, 0) + jnp.where((c == 0) & (zh == 0), 1, 0)
-        pl.semaphore_wait(barrier, 23 + 6 - 2 * c - mine)
+        pl.semaphore_wait(barrier, 8 + 6 - 2 * c)
+        tell(0)
 
     peer_copy = pltpu.make_async_remote_copy(
         src_ref=ordered.at[other],
@@ -186,22 +218,25 @@
         peer_copy.start()
 
     with jax.named_scope("p04table"):
-        loads[1].wait()
-        loads[2].wait()
+        told(0)
+        tell(1)
 
         @pl.loop(0, 64)
         def _(n):
-            h = lax.div(n, 32)
-            at_row = pl.multiple_of(lax.rem(n, 32) * 16, 16)
+            at_row = pl.multiple_of(n * 16, 16)
             for q in range(4):
                 at = slice(q * 256, (q + 1) * 256)
-                cos_top = top[pl.ds(n, 1), at]
-                sin_top = top[pl.ds(64 + n, 1), at]
-                cos_low = low[0:16, at]
-                sin_low = low[16:32, at]
-                table[h, pl.ds(at_row, 16), at] = (cos_top * cos_low - sin_top * sin_low).astype(BF16)
-                table[h, pl.ds(512 + at_row, 16), at] = (sin_top * cos_low + cos_top * sin_low).astype(BF16)
-
+                to = slice((q % 2) * 256, (q % 2) * 256 + 256)
+                to_sin = slice(512 + (q % 2) * 256, 512 + (q % 2) * 256 + 256)
+                cos_top = angles[1, pl.ds(n, 1), at]
+                sin_top = angles[1, pl.ds(64 + n, 1), at]
+                cos_low = angles[1, 128:144, at]
+                sin_low = angles[1, 144:160, at]
+                turned[q // 2, pl.ds(at_row, 16), to] = (cos_top * cos_low - sin_top * sin_low).astype(BF16)
+                turned[q // 2, pl.ds(at_row, 16), to_sin] = (sin_top * cos_low + cos_top * sin_low).astype(BF16)
+
+        told(1)
+        tell(2)
         loads[3].wait()
         for n in range(16):
             model_rows[n * 4 : (n + 1) * 4, :] = model[0, n // 4, n % 4].astype(F32)
@@ -218,6 +253,8 @@
     with jax.named_scope("p05fwdwait"):
         for q in range(5):
             pltpu.make_async_copy(partner.at[q], partner.at[q], come_sem.at[q]).wait()
+        told(2)
+        tell(3)
 
     def cross_of(t):
         @pl.loop(0, 4)
@@ -269,13 +306,10 @@
         gather(left.at[0])
 
     with jax.named_scope("p07lag"):
-        @pl.loop(0, 4)
-        def _(q):
-            at = pl.multiple_of(q * 256, 256)
-            lagged[:, pl.ds(at, 256)] = jnp.dot(
-                left[0], table[c, :, pl.ds(at, 256)], preferred_element_type=F32
-            )
-
+        lagged[...] = jnp.dot(left[0], table[c], preferred_element_type=F32)
+
+        loads[4].wait()
+        loads[5].wait()
         row = lax.broadcasted_iota(jnp.int32, (64, 1), 0)
         offset = lax.div(row, 16)
         start = jnp.zeros((64, 1), jnp.int32)
@@ -286,18 +320,10 @@
         diagonal = (lax.rem(lax.div(row, 4), 4) == lax.rem(row, 4)) & (offset == 0) & (lay == 0)
         end = jnp.where(diagonal, 0, end)
         left_copy.wait()
-
-        @pl.loop(0, 4)
-        def _(q):
-            at = pl.multiple_of(q * 256, 256)
-            value = lagged[:, pl.ds(at, 256)] + jnp.dot(
-                left[1], table[other, :, pl.ds(at, 256)], preferred_element_type=F32
-            )
-            lag = at + lax.broadcasted_iota(jnp.int32, (64, 256), 1)
-            keep = (lag >= start) & (lag < end)
-            misfit[:, pl.ds(at, 256)] = jnp.where(
-                keep, value - model_rows[:, pl.ds(at, 256)], 0.0
-            ).astype(BF16)
+        value = lagged[...] + jnp.dot(left[1], table[other], preferred_element_type=F32)
+        lag = lax.broadcasted_iota(jnp.int32, (64, 1024), 1)
+        keep = (lag >= start) & (lag < end)
+        misfit[...] = jnp.where(keep, value - model_rows[...], 0.0).astype(BF16)
 
     resp_copy = pltpu.make_async_remote_copy(
         src_ref=resp_out,
@@ -309,15 +335,7 @@
     )
 
     def respond(h, into):
-        @pl.loop(0, 4)
-        def _(q):
-            at = pl.multiple_of(q * 256, 256)
-            into[:, pl.ds(at, 256)] = lax.dot_general(
-                misfit[...],
-                table[h, pl.ds(at, 256), :],
-                (((1,), (1,)), ((), ())),
-                preferred_element_type=F32,
-            ).astype(BF16)
+        into[...] = jnp.dot(misfit[...], turned[h], preferred_element_type=F32).astype(BF16)
 
     def spread(n, t):
         for p in range(2):
@@ -326,50 +344,55 @@
                     n, :, p * 512 + k * 128 : p * 512 + (k + 1) * 128
                 ].astype(F32)
 
-    with jax.named_scope("p08resp"):
-        respond(other, resp_out)
-        resp_copy.start()
-        respond(c, resp.at[0])
-        spread(0, c)
-        resp_copy.wait()
-        spread(1, other)
-
-    with jax.named_scope("p09terms"):
-
+    def terms_of(t):
         @pl.loop(0, 4)
         def _(w):
             at_u = [pl.multiple_of(((p * 4 + w) * 4) * 8, 8) for p in range(2)]
             at_v = [pl.multiple_of((p * 4 + w) * 16, 16) for p in range(2)]
-            u = [
-                [first[t, pl.ds(at_u[p] + i * 8, 8), :] for p in range(2) for i in range(4)]
-                for t in range(2)
-            ]
-            total = [[jnp.zeros((8, 128), F32)] * 8 for t in range(2)]
-            for q in range(5):
-                v = [partner[q, pl.ds(at_v[p], 16), :].astype(F32) for p in range(2)]
+            u = [first[t, pl.ds(at_u[p] + i * 8, 8), :] for p in range(2) for i in range(4)]
+            total = [jnp.zeros((8, 128), F32)] * 8
+            for s in range(4):
+                v = [partner[t + s, pl.ds(at_v[p], 16), :].astype(F32) for p in range(2)]
                 for jp in range(2):
                     v_re = v[0][jp * 8 : jp * 8 + 8]
                     v_im = v[1][jp * 8 : jp * 8 + 8]
                     part_re = jnp.zeros((8, 128), F32)
                     part_im = jnp.zeros((8, 128), F32)
-                    for t in range(2):
-                        s = q - t
-                        if not 0 <= s < 4:
-                            continue
-                        for i in range(4):
-                            at = ((s * 4 + i) * 2 + jp) * 8
-                            a = resp_rows[t, at : at + 8, :]
-                            b = resp_rows[t, 256 + at : 256 + at + 8, :]
-                            total[t][i] = total[t][i] + (a * v_re - b * v_im)
-                            total[t][4 + i] = total[t][4 + i] + (a * v_im + b * v_re)
-                            part_re = part_re + (a * u[t][i] + b * u[t][4 + i])
-                            part_im = part_im + (a * u[t][4 + i] - b * u[t][i])
-                    part[q, pl.ds(at_v[0] + jp * 8, 8), :] = part_re
-                    part[q, pl.ds(at_v[1] + jp * 8, 8), :] = part_im
-            for t in range(2):
-                for p in range(2):
                     for i in range(4):
-                        own[t, pl.ds(((p * 4 + i) * 4 + w) * 8, 8), :] = total[t][p * 4 + i]
+                        at = ((s * 4 + i) * 2 + jp) * 8
+                        a = resp_rows[t, at : at + 8, :]
+                        b = resp_rows[t, 256 + at : 256 + at + 8, :]
+                        total[i] = total[i] + (a * v_re - b * v_im)
+                        total[4 + i] = total[4 + i] + (a * v_im + b * v_re)
+                        part_re = part_re + (a * u[i] + b * u[4 + i])
+                        part_im = part_im + (a * u[4 + i] - b * u[i])
+                    part[t, s, pl.ds(at_v[0] + jp * 8, 8), :] = part_re
+                    part[t, s, pl.ds(at_v[1] + jp * 8, 8), :] = part_im
+            for p in range(2):
+                for i in range(4):
+                    own[t, pl.ds(((p * 4 + i) * 4 + w) * 8, 8), :] = total[p * 4 + i]
+
+    with jax.named_scope("p08resp"):
+
+        @pl.when(c == 0)
+        def _():
+            respond(0, resp.at[0])
+            respond(1, resp_out)
+            resp_copy.start()
+
+        @pl.when(c == 1)
+        def _():
+            respond(0, resp_out)
+            resp_copy.start()
+            respond(1, resp.at[0])
+
+        spread(0, c)
+        terms_of(c)
+        resp_copy.wait()
+
+    with jax.named_scope("p09terms"):
+        spread(1, other)
+        terms_of(other)
 
     with jax.named_scope("p10pack"):
         for k in range(4):
@@ -378,7 +401,8 @@
                     own[t, pl.ds(k, 32, stride=8), :] + own[t, pl.ds(4 + k, 32, stride=8), :]
                 ).astype(BF16)
             for q in range(5):
-                outbox[k, q] = part[q, pl.ds(k, 32, stride=4), :].astype(BF16)
+                value = [part[t, q - t, pl.ds(k, 32, stride=4), :] for t in range(2) if 0 <= q - t < 4]
+                outbox[k, q] = (value[0] if len(value) == 1 else value[0] + value[1]).astype(BF16)
 
     def across(t):
         to = lax.rem(x + t, 4)
@@ -404,7 +428,7 @@
                 device_id_type=MESH,
             ).start()
 
-        if m in (0, 17, 18):
+        if isinstance(m, int) and m in (0, 17, 18):
             away = elsewhere(to)
             pl.when(away)(start)
 
@@ -419,13 +443,16 @@
             across(t).start()
         keep_copy = pltpu.make_async_copy(outbox.at[x], inbox.at[x], x_recv.at[x])
         keep_copy.start()
-        for n in range(4):
+        told(3)
+        tell(4)
+        told(4)
+        for t in (0, 1, 3, 2):
+            n = lax.rem(x + t, 4)
             pltpu.make_async_copy(inbox.at[n], inbox.at[n], x_recv.at[n]).wait()
-
-    with jax.named_scope("p12merge"):
-        for n in range(4):
             for r in range(1, 4):
                 deliver(inbox.at[n, r], 4 * n + r)
+
+    with jax.named_scope("p12merge"):
         deliver(inbox.at[0, 0], 0)
         deliver(inbox.at[3, 4], 16)
         for t in range(2):
@@ -497,20 +524,21 @@
 
 
 def local(spectra, model_corr, window_start, window_end, station_slot):
-    top, low = angle_parts()
-    smem = pl.BlockSpec(memory_space=pltpu.SMEM)
+    angles = angle_parts()
     hbm = pl.BlockSpec(memory_space=pl.ANY)
     dma = pltpu.SemaphoreType.DMA
     return pl.pallas_call(
         kernel,
-        out_shape=jax.ShapeDtypeStruct((2, 4, 4, 128), F32),
-        in_specs=[smem] * 3 + [hbm] * 4,
+        out_shape=pltpu.VMEM((2, 4, 4, 128), F32),
+        in_specs=[hbm] * 6,
         out_specs=pl.BlockSpec(memory_space=pltpu.VMEM),
         scratch_shapes=[
+            pltpu.SMEM((1, 4), jnp.int32),
+            pltpu.SMEM((1, 4), jnp.int32),
+            pltpu.SMEM((1, 4), jnp.int32),
             pltpu.VMEM((2, 4, 4, 1024), BF16),
             pltpu.VMEM((1, 4, 4, 4, 1024), BF16),
-            pltpu.VMEM((128, 1024), F32),
-            pltpu.VMEM((32, 1024), F32),
+            pltpu.VMEM((2, 160, 1024), F32),
             pltpu.VMEM((256, 128), F32),
             pltpu.VMEM((2, 128, 128), F32),
             pltpu.VMEM((2, 128, 128), BF16),
@@ -521,6 +549,7 @@
             pltpu.VMEM((2, 64, 1024), BF16),
             pltpu.VMEM((64, 1024), BF16),
             pltpu.VMEM((2, 1024, 1024), BF16),
+            pltpu.VMEM((2, 1024, 1024), BF16),
             pltpu.VMEM((64, 1024), F32),
             pltpu.VMEM((64, 1024), F32),
             pltpu.VMEM((64, 1024), BF16),
@@ -528,18 +557,17 @@
             pltpu.VMEM((64, 1024), BF16),
             pltpu.VMEM((2, 512, 128), F32),
             pltpu.VMEM((2, 256, 128), F32),
-            pltpu.VMEM((5, 128, 128), F32),
+            pltpu.VMEM((2, 4, 128, 128), F32),
             pltpu.VMEM((4, 7, 32, 128), BF16),
             pltpu.VMEM((4, 7, 32, 128), BF16),
             pltpu.VMEM((5, 32, 128), BF16),
             pltpu.VMEM((20, 32, 128), BF16),
-            dma((4,)), dma((3,)), dma((3,)), dma((6,)), dma((5,)), dma((3,)), dma((4,)), dma, dma,
+            dma((6,)), pltpu.SemaphoreType.REGULAR((5,)), dma((3,)), dma((3,)), dma((6,)), dma((5,)), dma((3,)), dma((4,)), dma, dma,
         ],
         compiler_params=pltpu.CompilerParams(has_side_effects=True, collective_id=0),
         name="adjoint",
     )(
-        window_start, window_end, station_slot, spectra, model_corr,
-        jnp.asarray(top), jnp.asarray(low),
+        window_start, window_end, station_slot, spectra, model_corr, jnp.asarray(angles),
     )
 
 

time: 48 us -> 43.2 us (0.900)
  Pallas kernels: 46.1 us -> 42.5 us
  local copies, waits for them, and re-layouts: 1.32 us -> 0.61 us
    pallas_call x1, Pallas kernels: 46.1 us -> 42.5 us  [local(): pl.pallas_call(kernel, out_shape=pltpu.VMEM((2, 4, 4, 128), F32), in_spec...]
    unnamed x1, local copies, waits for them, and re-layouts: 1.32 us -> 0.61 us
where the time goes in v3:
time: 43.2 us; the launch traced here: 43.1 us
  Pallas kernels  42.5 us (98%)
  local copies, waits for them, and re-layouts  0.61 us (1%)
    pallas_call x1, Pallas kernels, local(): pl.pallas_call(kernel, out_shape=pltpu.VMEM((2, 4, 4, 128), F32), in_spec...  42.5 us

profile of v3, /device:TPU:1, one launch (start us, length us, event | category | flops | bytes accessed | tf_op | source)
XLA Modules:
  0.0 43.1 jit_solution(17634505974462944910)
XLA Ops:
  0.0 42.5 %adjoint.1 = f32[2,4,4,128]{3,2,1,0:T(4,128)S(1)} custom-call(s32[1,4]{1,0:T(1,128)} %starts_hbm.1, s32[1,4]{1,0:T(1,128)} %ends_hbm.1, s32[1,4]{1,0:T(1,128)} %slots_hbm.1, bf16[2,4,4,1024]{3,2,1,0:T(4,128)(2,1)} %spec_hbm.1, bf16[1,4,4,4,1024]{4,3,2,1,0:T(4,128)(2,1)} %model_hbm.1, f32[2,160,1024]{2,1,0:T(8,128)} %constant.2.clone.angles_hbm), custom_call_target="tpu_custom_call" | custom-call | tf_op jit(solution)/shard_map/adjoint/pallas_call | solution.py:530
  42.5 0.6 %copy.8 = f32[2,4,4,128]{3,2,1,0:T(4,128)} copy(f32[2,4,4,128]{3,2,1,0:T(4,128)S(1)} %adjoint.1) | data formatting | bytes 32768

commit v4 on v3

--- a/solution.py
+++ b/solution.py
@@ -15,7 +15,13 @@
 SOURCE = [[3, 1, 0, 0, 0], [2, 0, 1, 1, 1], [3, 2, 2, 2, 1], [3, 3, 0, 3, 2]]
 AHEAD = [[0, 0, 1, 1, 2], [2, 2, 3, 3, -4], [4, 4, -3, -3, -2], [-2, -2, -1, -1, 0]]
 SENT = [
-    [[(x, q) for x in range(4) for q in range(core, 5, 2) if SOURCE[x][q] == source] for core in range(2)]
+    [
+        sorted(
+            [(x, q) for x in range(4) for q in range(core, 5, 2) if SOURCE[x][q] == source],
+            key=lambda to: -abs(AHEAD[to[0]][to[1]]),
+        )
+        for core in range(2)
+    ]
     for source in range(4)
 ]
 
@@ -104,6 +110,22 @@
     def elsewhere(to):
         return (to[0] != blk) | (to[1] != lay)
 
+    with jax.named_scope("p00greet"):
+        barrier = pltpu.get_barrier_semaphore()
+
+        def greet(to):
+            pl.semaphore_signal(barrier, inc=1, device_id=to, device_id_type=MESH)
+
+        for q in range(5):
+            greet(sender(q))
+        greet(peer)
+        for t in range(1, 4):
+            greet((blk, zh * 4 + lax.rem(x + t, 4)))
+        for d in (-4, -3, -2, -1, 1, 2, 3, 4):
+            greet(device(x, y, lax.rem(z + d + 16, 16), c))
+        for d in (1, 2, 3):
+            greet(device(x, y + d, z, c))
+
     loads = [
         pltpu.make_async_copy(spec_hbm, spec, load_sem.at[0]),
         pltpu.make_async_copy(slots_hbm, slots, load_sem.at[1]),
@@ -115,33 +137,18 @@
     for load in loads:
         load.start()
 
-    barrier = pltpu.get_barrier_semaphore()
-
-    def greet(to):
-        pl.semaphore_signal(barrier, inc=1, device_id=to, device_id_type=MESH)
-
-    for q in range(5):
-        greet(sender(q))
-    greet(peer)
-    for t in range(1, 4):
-        greet((blk, zh * 4 + lax.rem(x + t, 4)))
     near = [
-        [device(x, y + d, z, c) for d in (-1, 1)],
-        [device(x, y, lax.rem(z + d + 16, 16), c) for d in (-1, 1)],
-        [device(x, y, lax.rem(z + d + 16, 16), c) for d in (-2, 2)],
+        [peer],
+        [device(x, y + d, z, c) for d in (1, 2, 3)],
         [device(x, y, lax.rem(z + d + 16, 16), c) for d in (-4, 4)],
-        [device(x, y + d, z, c) for d in (-1, 1)],
     ]
-    for pair in near[:2]:
-        for to in pair:
-            greet(to)
 
     def tell(n):
         for to in near[n]:
             pl.semaphore_signal(ring_sem.at[n], inc=1, device_id=to, device_id_type=MESH)
 
     def told(n):
-        pl.semaphore_wait(ring_sem.at[n], 2)
+        pl.semaphore_wait(ring_sem.at[n], len(near[n]))
 
     with jax.named_scope("p01order"):
         loads[0].wait()
@@ -165,7 +172,43 @@
         for h in range(2):
             ordered[h] = halves[h].astype(BF16)
 
-    with jax.named_scope("p01table"):
+    with jax.named_scope("p02barrier"):
+        pl.semaphore_wait(barrier, 15 + 6 - 2 * c)
+
+    peer_copy = pltpu.make_async_remote_copy(
+        src_ref=ordered.at[other],
+        dst_ref=peer_half,
+        send_sem=peer_send.at[0],
+        recv_sem=peer_recv.at[0],
+        device_id=peer,
+        device_id_type=MESH,
+    )
+
+    def forward(n, core):
+        to, q = receiver(n, core)
+        return pltpu.make_async_remote_copy(
+            src_ref=ordered.at[core],
+            dst_ref=partner.at[q],
+            send_sem=go_sem.at[2 * n + core],
+            recv_sem=come_sem.at[q],
+            device_id=to,
+            device_id_type=MESH,
+        )
+
+    with jax.named_scope("p03fwd"):
+        for n in range(2):
+            for core in range(2):
+                forward(n, core).start()
+
+        @pl.when(c == 0)
+        def _():
+            for core in range(2):
+                forward(2, core).start()
+
+        peer_copy.start()
+        tell(0)
+
+    with jax.named_scope("p04table"):
         loads[2].wait()
 
         @pl.loop(0, 64)
@@ -181,43 +224,6 @@
                 table[h, pl.ds(at_row, 16), at] = (cos_top * cos_low - sin_top * sin_low).astype(BF16)
                 table[h, pl.ds(512 + at_row, 16), at] = (sin_top * cos_low + cos_top * sin_low).astype(BF16)
 
-    with jax.named_scope("p02barrier"):
-        pl.semaphore_wait(barrier, 8 + 6 - 2 * c)
-        tell(0)
-
-    peer_copy = pltpu.make_async_remote_copy(
-        src_ref=ordered.at[other],
-        dst_ref=peer_half,
-        send_sem=peer_send.at[0],
-        recv_sem=peer_recv.at[0],
-        device_id=peer,
-        device_id_type=MESH,
-    )
-
-    def forward(n, core):
-        to, q = receiver(n, core)
-        return pltpu.make_async_remote_copy(
-            src_ref=ordered.at[core],
-            dst_ref=partner.at[q],
-            send_sem=go_sem.at[2 * n + core],
-            recv_sem=come_sem.at[q],
-            device_id=to,
-            device_id_type=MESH,
-        )
-
-    with jax.named_scope("p03fwd"):
-        for n in range(2):
-            for core in range(2):
-                forward(n, core).start()
-
-        @pl.when(c == 0)
-        def _():
-            for core in range(2):
-                forward(2, core).start()
-
-        peer_copy.start()
-
-    with jax.named_scope("p04table"):
         told(0)
         tell(1)
 
@@ -253,8 +259,6 @@
     with jax.named_scope("p05fwdwait"):
         for q in range(5):
             pltpu.make_async_copy(partner.at[q], partner.at[q], come_sem.at[q]).wait()
-        told(2)
-        tell(3)
 
     def cross_of(t):
         @pl.loop(0, 4)
@@ -404,16 +408,29 @@
                 value = [part[t, q - t, pl.ds(k, 32, stride=4), :] for t in range(2) if 0 <= q - t < 4]
                 outbox[k, q] = (value[0] if len(value) == 1 else value[0] + value[1]).astype(BF16)
 
-    def across(t):
+    def far(n, q):
+        if q == 5:
+            return c != zh
+        ahead = 2 * n + q // 2
+        steps = lax.rem(8 * c + lax.rem(z + ahead, 8) - z + 16, 16)
+        return (steps > 4) & (steps < 12)
+
+    def rows(ref, n, q):
+        return ref.at[n, 5:7] if q == 5 else ref.at[n, q]
+
+    def across(t, q):
         to = lax.rem(x + t, 4)
         return pltpu.make_async_remote_copy(
-            src_ref=outbox.at[to],
-            dst_ref=inbox.at[x],
-            send_sem=x_send.at[t - 1],
-            recv_sem=x_recv.at[x],
+            src_ref=rows(outbox, to, q),
+            dst_ref=rows(inbox, x, q),
+            send_sem=x_send,
+            recv_sem=x_recv.at[x, q],
             device_id=(blk, zh * 4 + to),
             device_id_type=MESH,
         )
+
+    def here(n, q):
+        return pltpu.make_async_copy(rows(inbox, n, q), rows(inbox, n, q), x_recv.at[n, q])
 
     def deliver(source, m):
         to, slot = target(m)
@@ -438,34 +455,48 @@
         else:
             start()
 
+    def when_far(now, n, q):
+        return pl.when(far(n, q) if now else jnp.logical_not(far(n, q)))
+
     with jax.named_scope("p11x"):
-        for t in (2, 1, 3):
-            across(t).start()
-        keep_copy = pltpu.make_async_copy(outbox.at[x], inbox.at[x], x_recv.at[x])
-        keep_copy.start()
-        told(3)
-        tell(4)
-        told(4)
-        for t in (0, 1, 3, 2):
-            n = lax.rem(x + t, 4)
-            pltpu.make_async_copy(inbox.at[n], inbox.at[n], x_recv.at[n]).wait()
-            for r in range(1, 4):
-                deliver(inbox.at[n, r], 4 * n + r)
-
-    with jax.named_scope("p12merge"):
-        deliver(inbox.at[0, 0], 0)
-        deliver(inbox.at[3, 4], 16)
-        for t in range(2):
-            value = inbox[0, 5 + t].astype(F32)
+        for now in (True, False):
+            for t in (2, 1, 3):
+                for q in (5, 0, 1, 2, 3, 4):
+                    when_far(now, x, q)(across(t, q).start)
+        for q in range(6):
+            pltpu.make_async_copy(rows(outbox, x, q), rows(inbox, x, q), x_recv.at[x, q]).start()
+        told(2)
+
+    for now in (True, False):
+        with jax.named_scope("p12relay" + str(int(now))):
+            for n in (0, 3, 1, 2):
+                if n == 1:
+                    @when_far(now, 0, 5)
+                    def _():
+                        for n in range(4):
+                            here(n, 5).wait()
+                        for t in range(2):
+                            value = inbox[0, 5 + t].astype(F32)
+                            for n in range(1, 4):
+                                value = value + inbox[n, 5 + t].astype(F32)
+                            merged[3 + t] = value.astype(BF16)
+                            deliver(merged.at[3 + t], 17 + t)
+
+                for q in {0: (0, 1, 2, 3), 3: (4, 3, 2, 1), 1: (1, 2, 3), 2: (3, 2, 1)}[n]:
+
+                    @when_far(now, n, q)
+                    def _():
+                        here(n, q).wait()
+                        deliver(inbox.at[n, q], 4 * n + q)
+
             for n in range(1, 4):
-                value = value + inbox[n, 5 + t].astype(F32)
-            merged[3 + t] = value.astype(BF16)
-        for n in range(1, 4):
-            merged[n - 1] = (inbox[n, 0].astype(F32) + inbox[n - 1, 4].astype(F32)).astype(BF16)
-        for n in range(1, 4):
-            deliver(merged.at[n - 1], 4 * n)
-        for t in range(2):
-            deliver(merged.at[3 + t], 17 + t)
+
+                @when_far(now, n, 0)
+                def _():
+                    here(n, 0).wait()
+                    here(n - 1, 4).wait()
+                    merged[n - 1] = (inbox[n, 0].astype(F32) + inbox[n - 1, 4].astype(F32)).astype(BF16)
+                    deliver(merged.at[n - 1], 4 * n)
 
     with jax.named_scope("p13wait"):
 
@@ -513,8 +544,7 @@
             for core in range(2):
                 forward(2, core).wait_send()
 
-        for t in range(1, 4):
-            across(t).wait_send()
+        pltpu.make_async_copy(outbox.at[0:3], outbox.at[0:3], x_send).wait()
         for n in range(3):
 
             @pl.when(mine == n)
@@ -562,7 +592,7 @@
             pltpu.VMEM((4, 7, 32, 128), BF16),
             pltpu.VMEM((5, 32, 128), BF16),
             pltpu.VMEM((20, 32, 128), BF16),
-            dma((6,)), pltpu.SemaphoreType.REGULAR((5,)), dma((3,)), dma((3,)), dma((6,)), dma((5,)), dma((3,)), dma((4,)), dma, dma,
+            dma((6,)), pltpu.SemaphoreType.REGULAR((3,)), dma((3,)), dma((3,)), dma((6,)), dma((5,)), dma, dma((4, 6)), dma, dma,
         ],
         compiler_params=pltpu.CompilerParams(has_side_effects=True, collective_id=0),
         name="adjoint",

time: 43.2 us -> 43 us (level)
  no operation moved by 1% of the time
where the time goes in v4:
time: 43 us; the launch traced here: 42.9 us
  Pallas kernels  42.2 us (98%)
  local copies, waits for them, and re-layouts  0.61 us (1%)
    pallas_call x1, Pallas kernels, local(): pl.pallas_call(kernel, out_shape=pltpu.VMEM((2, 4, 4, 128), F32), in_spec...  42.2 us

profile of v4, /device:TPU:1, one launch (start us, length us, event | category | flops | bytes accessed | tf_op | source)
XLA Modules:
  0.0 42.9 jit_solution(15507430348515360146)
XLA Ops:
  0.0 42.2 %adjoint.1 = f32[2,4,4,128]{3,2,1,0:T(4,128)S(1)} custom-call(s32[1,4]{1,0:T(1,128)} %starts_hbm.1, s32[1,4]{1,0:T(1,128)} %ends_hbm.1, s32[1,4]{1,0:T(1,128)} %slots_hbm.1, bf16[2,4,4,1024]{3,2,1,0:T(4,128)(2,1)} %spec_hbm.1, bf16[1,4,4,4,1024]{4,3,2,1,0:T(4,128)(2,1)} %model_hbm.1, f32[2,160,1024]{2,1,0:T(8,128)} %constant.2.clone.angles_hbm), custom_call_target="tpu_custom_call" | custom-call | tf_op jit(solution)/shard_map/adjoint/pallas_call | solution.py:560
  42.3 0.6 %copy.8 = f32[2,4,4,128]{3,2,1,0:T(4,128)} copy(f32[2,4,4,128]{3,2,1,0:T(4,128)S(1)} %adjoint.1) | data formatting | bytes 32768

commit v5 on v4

--- a/solution.py
+++ b/solution.py
@@ -189,8 +189,8 @@
         return pltpu.make_async_remote_copy(
             src_ref=ordered.at[core],
             dst_ref=partner.at[q],
-            send_sem=go_sem.at[2 * n + core],
-            recv_sem=come_sem.at[q],
+            send_sem=go_sem,
+            recv_sem=come_sem,
             device_id=to,
             device_id_type=MESH,
         )
@@ -257,8 +257,7 @@
                 first[t, n * 8 + 4 : n * 8 + 8, :] = value
 
     with jax.named_scope("p05fwdwait"):
-        for q in range(5):
-            pltpu.make_async_copy(partner.at[q], partner.at[q], come_sem.at[q]).wait()
+        pltpu.make_async_copy(partner, partner, come_sem).wait()
 
     def cross_of(t):
         @pl.loop(0, 4)
@@ -408,29 +407,19 @@
                 value = [part[t, q - t, pl.ds(k, 32, stride=4), :] for t in range(2) if 0 <= q - t < 4]
                 outbox[k, q] = (value[0] if len(value) == 1 else value[0] + value[1]).astype(BF16)
 
-    def far(n, q):
-        if q == 5:
-            return c != zh
-        ahead = 2 * n + q // 2
-        steps = lax.rem(8 * c + lax.rem(z + ahead, 8) - z + 16, 16)
-        return (steps > 4) & (steps < 12)
-
-    def rows(ref, n, q):
-        return ref.at[n, 5:7] if q == 5 else ref.at[n, q]
-
-    def across(t, q):
+    def across(t):
         to = lax.rem(x + t, 4)
         return pltpu.make_async_remote_copy(
-            src_ref=rows(outbox, to, q),
-            dst_ref=rows(inbox, x, q),
+            src_ref=outbox.at[to],
+            dst_ref=inbox.at[x],
             send_sem=x_send,
-            recv_sem=x_recv.at[x, q],
+            recv_sem=x_recv.at[x],
             device_id=(blk, zh * 4 + to),
             device_id_type=MESH,
         )
 
-    def here(n, q):
-        return pltpu.make_async_copy(rows(inbox, n, q), rows(inbox, n, q), x_recv.at[n, q])
+    def here(n):
+        pltpu.make_async_copy(inbox.at[n], inbox.at[n], x_recv.at[n]).wait()
 
     def deliver(source, m):
         to, slot = target(m)
@@ -455,48 +444,31 @@
         else:
             start()
 
-    def when_far(now, n, q):
-        return pl.when(far(n, q) if now else jnp.logical_not(far(n, q)))
-
     with jax.named_scope("p11x"):
-        for now in (True, False):
-            for t in (2, 1, 3):
-                for q in (5, 0, 1, 2, 3, 4):
-                    when_far(now, x, q)(across(t, q).start)
-        for q in range(6):
-            pltpu.make_async_copy(rows(outbox, x, q), rows(inbox, x, q), x_recv.at[x, q]).start()
+        for t in (2, 1, 3):
+            across(t).start()
+        pltpu.make_async_copy(outbox.at[x], inbox.at[x], x_recv.at[x]).start()
         told(2)
 
-    for now in (True, False):
-        with jax.named_scope("p12relay" + str(int(now))):
-            for n in (0, 3, 1, 2):
-                if n == 1:
-                    @when_far(now, 0, 5)
-                    def _():
-                        for n in range(4):
-                            here(n, 5).wait()
-                        for t in range(2):
-                            value = inbox[0, 5 + t].astype(F32)
-                            for n in range(1, 4):
-                                value = value + inbox[n, 5 + t].astype(F32)
-                            merged[3 + t] = value.astype(BF16)
-                            deliver(merged.at[3 + t], 17 + t)
-
-                for q in {0: (0, 1, 2, 3), 3: (4, 3, 2, 1), 1: (1, 2, 3), 2: (3, 2, 1)}[n]:
-
-                    @when_far(now, n, q)
-                    def _():
-                        here(n, q).wait()
-                        deliver(inbox.at[n, q], 4 * n + q)
-
+    def merge(n):
+        merged[n - 1] = (inbox[n, 0].astype(F32) + inbox[n - 1, 4].astype(F32)).astype(BF16)
+        deliver(merged.at[n - 1], 4 * n)
+
+    with jax.named_scope("p12relay"):
+        for n, single in ((0, (0, 1, 2, 3)), (3, (4, 3, 2, 1)), (1, (3, 2, 1)), (2, (3, 2, 1))):
+            here(n)
+            for q in single:
+                deliver(inbox.at[n, q], 4 * n + q)
+            if n == 1:
+                merge(1)
+        merge(3)
+        merge(2)
+        for t in range(2):
+            value = inbox[0, 5 + t].astype(F32)
             for n in range(1, 4):
-
-                @when_far(now, n, 0)
-                def _():
-                    here(n, 0).wait()
-                    here(n - 1, 4).wait()
-                    merged[n - 1] = (inbox[n, 0].astype(F32) + inbox[n - 1, 4].astype(F32)).astype(BF16)
-                    deliver(merged.at[n - 1], 4 * n)
+                value = value + inbox[n, 5 + t].astype(F32)
+            merged[3 + t] = value.astype(BF16)
+            deliver(merged.at[3 + t], 17 + t)
 
     with jax.named_scope("p13wait"):
 
@@ -535,14 +507,12 @@
                     value = jnp.where(chosen[r][q][:4], row_of[r], value)
                 out[p, q] = value
 
-        for n in range(2):
-            for core in range(2):
-                forward(n, core).wait_send()
-
-        @pl.when(c == 0)
-        def _():
-            for core in range(2):
-                forward(2, core).wait_send()
+        for half in range(2):
+
+            @pl.when(c == half)
+            def _():
+                gone = table.at[0, 0 : 96 - 32 * half]
+                pltpu.make_async_copy(gone, gone, go_sem).wait()
 
         pltpu.make_async_copy(outbox.at[0:3], outbox.at[0:3], x_send).wait()
         for n in range(3):
@@ -592,7 +562,7 @@
             pltpu.VMEM((4, 7, 32, 128), BF16),
             pltpu.VMEM((5, 32, 128), BF16),
             pltpu.VMEM((20, 32, 128), BF16),
-            dma((6,)), pltpu.SemaphoreType.REGULAR((3,)), dma((3,)), dma((3,)), dma((6,)), dma((5,)), dma, dma((4, 6)), dma, dma,
+            dma((6,)), pltpu.SemaphoreType.REGULAR((3,)), dma((3,)), dma((3,)), dma, dma, dma, dma((4,)), dma, dma,
         ],
         compiler_params=pltpu.CompilerParams(has_side_effects=True, collective_id=0),
         name="adjoint",

time: 43 us -> 42 us (0.977); the launches traced: 42.9 us -> 41.4 us
  Pallas kernels: 42.2 us -> 40.8 us
    pallas_call x1, Pallas kernels: 42.2 us -> 40.8 us  [local(): pl.pallas_call(kernel, out_shape=pltpu.VMEM((2, 4, 4, 128), F32), in_spec...]
where the time goes in v5:
time: 42 us; the launch traced here: 41.4 us
  Pallas kernels  40.8 us (97%)
  local copies, waits for them, and re-layouts  0.61 us (1%)
    pallas_call x1, Pallas kernels, local(): pl.pallas_call(kernel, out_shape=pltpu.VMEM((2, 4, 4, 128), F32), in_spec...  40.8 us

profile of v5, /device:TPU:1, one launch (start us, length us, event | category | flops | bytes accessed | tf_op | source)
XLA Modules:
  0.0 41.4 jit_solution(9835058042034877417)
XLA Ops:
  0.0 40.8 %adjoint.1 = f32[2,4,4,128]{3,2,1,0:T(4,128)S(1)} custom-call(s32[1,4]{1,0:T(1,128)} %starts_hbm.1, s32[1,4]{1,0:T(1,128)} %ends_hbm.1, s32[1,4]{1,0:T(1,128)} %slots_hbm.1, bf16[2,4,4,1024]{3,2,1,0:T(4,128)(2,1)} %spec_hbm.1, bf16[1,4,4,4,1024]{4,3,2,1,0:T(4,128)(2,1)} %model_hbm.1, f32[2,160,1024]{2,1,0:T(8,128)} %constant.2.clone.angles_hbm), custom_call_target="tpu_custom_call" | custom-call | tf_op jit(solution)/shard_map/adjoint/pallas_call | solution.py:530
  40.8 0.6 %copy.8 = f32[2,4,4,128]{3,2,1,0:T(4,128)} copy(f32[2,4,4,128]{3,2,1,0:T(4,128)S(1)} %adjoint.1) | data formatting | bytes 32768

commit v6 on v5

--- a/solution.py
+++ b/solution.py
@@ -99,7 +99,9 @@
         from_y = y + lax.div(z + 2 * x + q // 2, 8)
         return device(choose(x, [SOURCE[s][q] for s in range(4)]), from_y, from_z, q % 2)
 
-    mine = jnp.where(c == zh, 1, 0) + jnp.where((c == 0) & (zh == 0), 1, 0)
+    mine = jnp.where(c == zh, 1, 0) + jnp.where((c == 0) & (zh == 0) & (x != 2), 1, 0)
+    over = lax.rem(x + 2, 4)
+    outer = (x == 0) | (x == 3)
 
     def target(m):
         if isinstance(m, int) and m >= 17:
@@ -141,6 +143,7 @@
         [peer],
         [device(x, y + d, z, c) for d in (1, 2, 3)],
         [device(x, y, lax.rem(z + d + 16, 16), c) for d in (-4, 4)],
+        [device(lax.rem(x + 2, 4), y, z, c)],
     ]
 
     def tell(n):
@@ -206,7 +209,7 @@
                 forward(2, core).start()
 
         peer_copy.start()
-        tell(0)
+        tell(3)
 
     with jax.named_scope("p04table"):
         loads[2].wait()
@@ -224,8 +227,8 @@
                 table[h, pl.ds(at_row, 16), at] = (cos_top * cos_low - sin_top * sin_low).astype(BF16)
                 table[h, pl.ds(512 + at_row, 16), at] = (sin_top * cos_low + cos_top * sin_low).astype(BF16)
 
-        told(0)
-        tell(1)
+        told(3)
+        tell(0)
 
         @pl.loop(0, 64)
         def _(n):
@@ -241,8 +244,8 @@
                 turned[q // 2, pl.ds(at_row, 16), to] = (cos_top * cos_low - sin_top * sin_low).astype(BF16)
                 turned[q // 2, pl.ds(at_row, 16), to_sin] = (sin_top * cos_low + cos_top * sin_low).astype(BF16)
 
-        told(1)
-        tell(2)
+        told(0)
+        tell(1)
         loads[3].wait()
         for n in range(16):
             model_rows[n * 4 : (n + 1) * 4, :] = model[0, n // 4, n % 4].astype(F32)
@@ -255,6 +258,9 @@
                 value = raw[n * 4 : n * 4 + 4, :]
                 first[t, n * 8 : n * 8 + 4, :] = value
                 first[t, n * 8 + 4 : n * 8 + 8, :] = value
+
+        told(1)
+        tell(2)
 
     with jax.named_scope("p05fwdwait"):
         pltpu.make_async_copy(partner, partner, come_sem).wait()
@@ -409,9 +415,10 @@
 
     def across(t):
         to = lax.rem(x + t, 4)
+        some = slice(5, 7) if t == 2 else slice(0, 7)
         return pltpu.make_async_remote_copy(
-            src_ref=outbox.at[to],
-            dst_ref=inbox.at[x],
+            src_ref=outbox.at[to, some],
+            dst_ref=inbox.at[x, some],
             send_sem=x_send,
             recv_sem=x_recv.at[x],
             device_id=(blk, zh * 4 + to),
@@ -419,7 +426,29 @@
         )
 
     def here(n):
-        pltpu.make_async_copy(inbox.at[n], inbox.at[n], x_recv.at[n]).wait()
+        @pl.when(over == n)
+        def _():
+            pltpu.make_async_copy(inbox.at[n, 5:7], inbox.at[n, 5:7], x_recv.at[n]).wait()
+
+        @pl.when(over != n)
+        def _():
+            pltpu.make_async_copy(inbox.at[n], inbox.at[n], x_recv.at[n]).wait()
+
+    def straight(q):
+        m = 4 * x + q
+        slot = lax.div(m, 2) * 2 + zh
+        if q == 0:
+            slot = jnp.where(x == 0, zh, 20 + zh)
+        if q == 4:
+            slot = jnp.where(x == 0, 20 + zh, jnp.where(x == 3, 18 + zh, 22 + zh))
+        pltpu.make_async_remote_copy(
+            src_ref=outbox.at[over, q],
+            dst_ref=last.at[slot],
+            send_sem=z_send,
+            recv_sem=z_recv,
+            device_id=(lax.rem(16 * y + 2 * z + m, 64), c * 4 + over),
+            device_id_type=MESH,
+        ).start()
 
     def deliver(source, m):
         to, slot = target(m)
@@ -451,14 +480,30 @@
         told(2)
 
     def merge(n):
-        merged[n - 1] = (inbox[n, 0].astype(F32) + inbox[n - 1, 4].astype(F32)).astype(BF16)
+        head = jnp.where(over == n, 0.0, inbox[n, 0].astype(F32))
+        tail = jnp.where(over == n - 1, 0.0, inbox[n - 1, 4].astype(F32))
+        merged[n - 1] = (head + tail).astype(BF16)
         deliver(merged.at[n - 1], 4 * n)
 
     with jax.named_scope("p12relay"):
+        for q in range(5):
+            straight(q)
+        for q in (3, 2, 1):
+            deliver(outbox.at[x, q], 4 * x + q)
+        for n, m in ((0, 0), (3, 16)):
+
+            @pl.when(x == n)
+            def _():
+                deliver(outbox.at[n, m // 4], m)
+
         for n, single in ((0, (0, 1, 2, 3)), (3, (4, 3, 2, 1)), (1, (3, 2, 1)), (2, (3, 2, 1))):
             here(n)
-            for q in single:
-                deliver(inbox.at[n, q], 4 * n + q)
+
+            @pl.when((x != n) & (over != n))
+            def _():
+                for q in single:
+                    deliver(inbox.at[n, q], 4 * n + q)
+
             if n == 1:
                 merge(1)
         merge(3)
@@ -471,14 +516,11 @@
             deliver(merged.at[3 + t], 17 + t)
 
     with jax.named_scope("p13wait"):
-
-        @pl.when(c == 0)
-        def _():
-            pltpu.make_async_copy(last, last, z_recv).wait()
-
-        @pl.when(c == 1)
-        def _():
-            pltpu.make_async_copy(last.at[0:18], last.at[0:18], z_recv).wait()
+        for much, now in ((24, (c == 0) & outer), (22, (c == 0) & jnp.logical_not(outer)), (18, c == 1)):
+
+            @pl.when(now)
+            def _():
+                pltpu.make_async_copy(last.at[0:much], last.at[0:much], z_recv).wait()
 
     with jax.named_scope("p14sum"):
         total = last[0].astype(F32)
@@ -489,7 +531,11 @@
 
         @pl.when(c == 0)
         def _():
-            raw[0:32, :] = (total + last[18].astype(F32) + last[19].astype(F32)) * scale
+            rest = total
+            for n in range(18, 22):
+                rest = rest + last[n].astype(F32)
+            more = last[22].astype(F32) + last[23].astype(F32)
+            raw[0:32, :] = (rest + jnp.where(outer, more, 0.0)) * scale
 
         @pl.when(c == 1)
         def _():
@@ -514,12 +560,13 @@
                 gone = table.at[0, 0 : 96 - 32 * half]
                 pltpu.make_async_copy(gone, gone, go_sem).wait()
 
-        pltpu.make_async_copy(outbox.at[0:3], outbox.at[0:3], x_send).wait()
-        for n in range(3):
-
-            @pl.when(mine == n)
+        gone = table.at[0, 0:64]
+        pltpu.make_async_copy(gone, gone, x_send).wait()
+        for n in range(18, 22):
+
+            @pl.when(jnp.where(outer, 21, 20) - mine == n)
             def _():
-                gone = last.at[0 : 19 - n]
+                gone = last.at[0:n]
                 pltpu.make_async_copy(gone, gone, z_send).wait()
 
 
@@ -561,8 +608,8 @@
             pltpu.VMEM((4, 7, 32, 128), BF16),
             pltpu.VMEM((4, 7, 32, 128), BF16),
             pltpu.VMEM((5, 32, 128), BF16),
-            pltpu.VMEM((20, 32, 128), BF16),
-            dma((6,)), pltpu.SemaphoreType.REGULAR((3,)), dma((3,)), dma((3,)), dma, dma, dma, dma((4,)), dma, dma,
+            pltpu.VMEM((24, 32, 128), BF16),
+            dma((6,)), pltpu.SemaphoreType.REGULAR((4,)), dma((3,)), dma((3,)), dma, dma, dma, dma((4,)), dma, dma,
         ],
         compiler_params=pltpu.CompilerParams(has_side_effects=True, collective_id=0),
         name="adjoint",

time: 42 us -> 41.1 us (0.979)
  Pallas kernels: 40.8 us -> 40.3 us
    pallas_call x1, Pallas kernels: 40.8 us -> 40.3 us  [local(): pl.pallas_call(kernel, out_shape=pltpu.VMEM((2, 4, 4, 128), F32), in_spec...]
where the time goes in v6:
time: 41.1 us; the launch traced here: 40.9 us
  Pallas kernels  40.3 us (98%)
  local copies, waits for them, and re-layouts  0.61 us (1%)
    pallas_call x1, Pallas kernels, local(): pl.pallas_call(kernel, out_shape=pltpu.VMEM((2, 4, 4, 128), F32), in_spec...  40.3 us

profile of v6, /device:TPU:1, one launch (start us, length us, event | category | flops | bytes accessed | tf_op | source)
XLA Modules:
  0.0 40.9 jit_solution(1161147188149174403)
XLA Ops:
  0.0 40.3 %adjoint.1 = f32[2,4,4,128]{3,2,1,0:T(4,128)S(1)} custom-call(s32[1,4]{1,0:T(1,128)} %starts_hbm.1, s32[1,4]{1,0:T(1,128)} %ends_hbm.1, s32[1,4]{1,0:T(1,128)} %slots_hbm.1, bf16[2,4,4,1024]{3,2,1,0:T(4,128)(2,1)} %spec_hbm.1, bf16[1,4,4,4,1024]{4,3,2,1,0:T(4,128)(2,1)} %model_hbm.1, f32[2,160,1024]{2,1,0:T(8,128)} %constant.2.clone.angles_hbm), custom_call_target="tpu_custom_call" | custom-call | tf_op jit(solution)/shard_map/adjoint/pallas_call | solution.py:577
  40.3 0.6 %copy.8 = f32[2,4,4,128]{3,2,1,0:T(4,128)} copy(f32[2,4,4,128]{3,2,1,0:T(4,128)S(1)} %adjoint.1) | data formatting | bytes 32768
